TPU v7x, 128 devices: a whole 4x4x4 slice. The times are simulated.
128 devices in a mesh: dp: 2 (over core), tensor: 64 (over x, z, y).
Axes of the slice: x: 4, y: 4, z: 4, core: 2. Of those that a mesh axis runs over, the one named last changes fastest.
Arguments:
- hidden: bfloat16 [2048, 4096], P(('dp', 'tensor')), parts along dimension 0
- norm_gain: float32 [4096], replicated, may hold values from 0.3 to 3
- head_weight: bfloat16 [256512, 4096], P(('dp', 'tensor')), parts along dimension 0
- targets: int32 [2048], P(('dp', 'tensor')), parts along dimension 0, may hold values from 0 to 128255
- lengths: int32 [24], P('dp'), parts along dimension 0, may hold values from 1 to 256, as said below
- offsets: int32 [24], P('dp'), parts along dimension 0, may hold values from 0 to 1023, as said below
- loss_mask: int32 [2048], P(('dp', 'tensor')), parts along dimension 0, may hold values from 0 to 1, as said below
Outputs:
- token_logprob: float32 [2048], P(('dp', 'tensor')), parts along dimension 0
- token_entropy: float32 [2048], P(('dp', 'tensor')), parts along dimension 0
- sequence_score: float32 [24], P('dp'), parts along dimension 0
There are 2 independent parts, one for each index of `dp`. A program takes and returns all parts, laid end to end along the dimension named above; an argument that names none is the same for every part. Nothing has to cross between parts.
Inputs may be any that keep to these rules, and one draw needn't show every extreme that they name: `lengths`: responses lie in order and do not intersection within the 1024 rows; one has length exactly 256. offsets[k] + lengths[k] <= offsets[k+1], and the last response ends within the pack. `loss_mask`: ones only inside responses; the 16 rows of one index of tensor hold at most 10 ones, exactly 10 on some index.
All inputs are finite; a program needn't handle non-finite values.
Results may differ from a plain program's by a relative error of at most 0.0065.
The roundings to bfloat16 on the way count: a program that leaves them out, or rounds other values in their place, can miss the bound.
Values may be sent and summed in bfloat16 or wider, within the bound.
No kernel may reach another device: no remote copies, remote signals or barrier semaphores. Data moves between devices by JAX's collectives and lax.ppermute only.
A program may use at most 128 MiB of HBM per device.

v0:
```python
import functools

import jax
import jax.numpy as jnp
import numpy as np
from jax import lax
from jax.experimental import pallas as pl
from jax.experimental.pallas import tpu as pltpu
from jax.sharding import PartitionSpec as P


epsilon = 1e-05

D = 4096
WIDE = D + 128
ROWS = 16
LIVE = 10
LINE = 4 * LIVE
ROWS_A = 24
ROWS_B = LINE - ROWS_A
VOCAB_TILE = 512


X, Z, Y = 0, 1, 2


def shifted_pairs(axis, step):
    pairs = []
    for index in range(64):
        coords = [index // 16, (index // 4) % 4, index % 4]
        coords[axis] = (coords[axis] - step) % 4
        pairs.append((index, coords[0] * 16 + coords[1] * 4 + coords[2]))
    return pairs


def from_ahead(value, axis, step):
    return lax.ppermute(value, "tensor", shifted_pairs(axis, step))


def three_ahead(value, axis):
    return [from_ahead(value, axis, 1), from_ahead(value, axis, 2), from_ahead(value, axis, 3)]


def in_order(pieces, own):
    return [lax.select_n((j - own) % 4, *pieces) for j in range(4)]


def pack_kernel(hidden_ref, targets_ref, mask_ref, out_ref):
    row = lax.broadcasted_iota(jnp.int32, (ROWS, ROWS), 0)
    other = lax.broadcasted_iota(jnp.int32, (ROWS, ROWS), 1)

    def total(chosen, values):
        return jnp.sum(jnp.where(chosen, values, 0), axis=1, keepdims=True)

    target = total(row == other, targets_ref[...])
    columns = [
        total(other < row, mask_ref[...]),
        target >> 12,
        (target >> 6) & 63,
        target & 63,
        row[:, 0:1],
        total(row == other, mask_ref[...]),
    ]
    lane = lax.broadcasted_iota(jnp.int32, (ROWS, 128), 1)
    extra = jnp.zeros((ROWS, 128), jnp.int32)
    for k, column in enumerate(columns):
        extra = jnp.where(lane == k, column, extra)
    out_ref[:, :D] = hidden_ref[...]
    out_ref[:, D:] = extra.astype(jnp.float32).astype(jnp.bfloat16)


def pack(hidden, targets, mask):
    vmem = pl.BlockSpec(memory_space=pltpu.VMEM)
    return pl.pallas_call(
        pack_kernel,
        name="pack",
        out_shape=jax.ShapeDtypeStruct((ROWS, WIDE), jnp.bfloat16),
        in_specs=[vmem] * 3,
        out_specs=vmem,
        cost_estimate=pl.CostEstimate(
            flops=ROWS * WIDE, bytes_accessed=4 * ROWS * WIDE, transcendentals=0
        ),
    )(hidden, targets, mask)


def prepare_kernel(own_ref, gain_ref, rows0, rows1, rows2, rows3, a_ref, b_ref):
    own = own_ref[0]
    normed, hots = [], []
    for k, ref in enumerate((rows0, rows1, rows2, rows3)):
        values = ref[:, :D].astype(jnp.float32)
        meansq = jnp.mean(values * values, axis=1, keepdims=True)
        scaled = values * lax.rsqrt(meansq + epsilon) * gain_ref[...]
        extra = ref[:, D:]
        normed.append(jnp.concatenate([scaled.astype(jnp.bfloat16), extra], axis=1))
        base = lax.rem(own + k, 4) * LIVE
        slot = extra[:, 0:1].astype(jnp.float32) + base.astype(jnp.float32)
        lane = lax.broadcasted_iota(jnp.int32, (ROWS, LINE), 1).astype(jnp.float32)
        live = extra[:, 5:6].astype(jnp.float32) > 0.5
        hots.append(jnp.where((slot == lane) & live, 1.0, 0.0).astype(jnp.bfloat16))
    hot = jnp.concatenate(hots, axis=0)
    rows = jnp.concatenate(normed, axis=0)
    line = lax.dot_general(
        hot, rows, (((0,), (0,)), ((), ())), preferred_element_type=jnp.float32
    ).astype(jnp.bfloat16)
    a_ref[...] = line[:ROWS_A]
    b_ref[...] = line[ROWS_A:]


def prepare(own, gain, pieces):
    vmem = pl.BlockSpec(memory_space=pltpu.VMEM)
    return pl.pallas_call(
        prepare_kernel,
        name="prepare",
        out_shape=(
            jax.ShapeDtypeStruct((ROWS_A, WIDE), jnp.bfloat16),
            jax.ShapeDtypeStruct((ROWS_B, WIDE), jnp.bfloat16),
        ),
        in_specs=[pl.BlockSpec(memory_space=pltpu.SMEM)] + [vmem] * 5,
        out_specs=(vmem, vmem),
        cost_estimate=pl.CostEstimate(
            flops=2 * 64 * LINE * WIDE, bytes_accessed=104 * WIDE * 2, transcendentals=64
        ),
    )(own, gain, *pieces)


def fetch(piece_refs, held, sems):
    copies, at = [], 0
    for k, ref in enumerate(piece_refs):
        rows = ref.shape[0]
        copies.append(pltpu.make_async_copy(ref, held.at[pl.ds(at, rows), :], sems.at[k]))
        at += rows
    for copy in copies:
        copy.start()
    for copy in copies:
        copy.wait()


def accumulate(step, vocab_rows, start, held, weight_ref, acc):
    rows = held.shape[0]

    @pl.when(step == 0)
    def _():
        acc[0] = jnp.full((rows, 128), -1e30, jnp.float32)
        acc[1] = jnp.zeros((rows, 128), jnp.float32)
        acc[2] = jnp.zeros((rows, 128), jnp.float32)
        acc[3] = jnp.zeros((rows, 128), jnp.float32)
        acc[4] = held[:, D:].astype(jnp.float32)

    tile = weight_ref.shape[0]
    scores = lax.dot_general(
        held[:, :D],
        weight_ref[...],
        (((1,), (1,)), ((), ())),
        preferred_element_type=jnp.float32,
    )
    lane = lax.broadcasted_iota(jnp.int32, (1, 128), 1)
    base = step * tile
    groups = [
        jnp.where(base + k + lane < vocab_rows, scores[:, k : k + 128], -1e30)
        for k in range(0, tile, 128)
    ]
    extra = acc[4]
    ids = extra[:, 1:2] * 4096.0 + extra[:, 2:3] * 64.0 + extra[:, 3:4]
    local_id = ids.astype(jnp.int32) - start
    local_id = jnp.where(local_id < vocab_rows, local_id, -1) - base
    before, sum_before = acc[0], acc[1]
    peak = functools.reduce(jnp.maximum, groups, before)
    shift_by = before - peak
    factor = jnp.exp(shift_by)
    total = factor * sum_before
    spread = factor * (acc[2] + shift_by * sum_before)
    picked = acc[3]
    for k, group in enumerate(groups):
        centred = group - peak
        expo = jnp.exp(centred)
        total = total + expo
        spread = spread + expo * centred
        picked = jnp.where(local_id == lane + 128 * k, group, picked)
    acc[0], acc[1], acc[2], acc[3] = peak, total, spread, picked


def near_kernel(vocab_rows, n_pieces, place_ref, *refs):
    weight_ref, acc, held, sems = refs[n_pieces:]
    step = pl.program_id(0)

    @pl.when(step == 0)
    def _():
        fetch(refs[:n_pieces], held, sems)

    accumulate(step, vocab_rows, place_ref[0], held, weight_ref, acc)


def rest_kernel(vocab_rows, n_pieces, na, nb, place_ref, *refs):
    near_ref, weight_ref, out_ref, info_ref, held, acc, all_rows, sems = refs[n_pieces:]
    step = pl.program_id(0)

    @pl.when(step == 0)
    def _():
        fetch(refs[:n_pieces], held, sems)

    accumulate(step, vocab_rows, place_ref[0], held, weight_ref, acc)

    @pl.when(step == pl.num_programs(0) - 1)
    def _():
        z, y = place_ref[1], place_ref[2]
        for k in range(4):
            to_a = pl.multiple_of(lax.rem(z + k, 4) * na, na)
            to_b = pl.multiple_of(4 * na + lax.rem(y + k, 4) * nb, nb)
            if k == 0:
                all_rows[:, pl.ds(to_a, na), :] = near_ref[:, :na, :]
                all_rows[:, pl.ds(to_b, nb), :] = near_ref[:, na:, :]
            else:
                at_a, at_b = (k - 1) * na, 3 * na + (k - 1) * nb
                all_rows[:, pl.ds(to_a, na), :] = acc[:, at_a : at_a + na, :]
                all_rows[:, pl.ds(to_b, nb), :] = acc[:, at_b : at_b + nb, :]
        for at in range(0, all_rows.shape[1], 128):
            peaks, sums, spreads, picks, extra = [
                all_rows[plane, at : at + 128, :].T for plane in range(5)
            ]
            top = jnp.max(peaks, axis=0, keepdims=True)
            shift_by = peaks - top
            factor = jnp.exp(shift_by)
            here = slice(at, at + 128)
            out_ref[0:1, here] = top
            out_ref[1:2, here] = jnp.sum(factor * sums, axis=0, keepdims=True)
            out_ref[2:3, here] = jnp.sum(
                factor * (spreads + shift_by * sums), axis=0, keepdims=True
            )
            out_ref[3:4, here] = jnp.sum(picks, axis=0, keepdims=True)
            info_ref[:, here] = extra[:8]


def score_cost(total, vocab_rows):
    return pl.CostEstimate(
        flops=2 * total * vocab_rows * D,
        bytes_accessed=vocab_rows * D * 2 + total * WIDE * 2,
        transcendentals=total * vocab_rows,
    )


def score_near(place, pieces, head_weight):
    total = sum(piece.shape[0] for piece in pieces)
    vocab_rows = head_weight.shape[0]
    return pl.pallas_call(
        functools.partial(near_kernel, vocab_rows, len(pieces)),
        name="near",
        grid=(pl.cdiv(vocab_rows, VOCAB_TILE),),
        out_shape=jax.ShapeDtypeStruct((5, total, 128), jnp.float32),
        in_specs=[pl.BlockSpec(memory_space=pltpu.SMEM)]
        + [pl.BlockSpec(memory_space=pl.ANY)] * len(pieces)
        + [pl.BlockSpec((VOCAB_TILE, D), lambda i: (i, 0))],
        out_specs=pl.BlockSpec((5, total, 128), lambda i: (0, 0, 0)),
        scratch_shapes=[
            pltpu.VMEM((total, WIDE), jnp.bfloat16),
            pltpu.SemaphoreType.DMA((len(pieces),)),
        ],
        cost_estimate=score_cost(total, vocab_rows),
    )(place, *pieces, head_weight)


def score_rest(place, pieces, near, head_weight, na, nb):
    total = sum(piece.shape[0] for piece in pieces)
    vocab_rows = head_weight.shape[0]
    return pl.pallas_call(
        functools.partial(rest_kernel, vocab_rows, len(pieces), na, nb),
        name="rest",
        grid=(pl.cdiv(vocab_rows, VOCAB_TILE),),
        out_shape=(
            jax.ShapeDtypeStruct((4, total + na + nb), jnp.float32),
            jax.ShapeDtypeStruct((8, total + na + nb), jnp.float32),
        ),
        in_specs=[pl.BlockSpec(memory_space=pltpu.SMEM)]
        + [pl.BlockSpec(memory_space=pl.ANY)] * len(pieces)
        + [pl.BlockSpec(near.shape, lambda i: (0, 0, 0)), pl.BlockSpec((VOCAB_TILE, D), lambda i: (i, 0))],
        out_specs=(
            pl.BlockSpec((4, total + na + nb), lambda i: (0, 0)),
            pl.BlockSpec((8, total + na + nb), lambda i: (0, 0)),
        ),
        scratch_shapes=[
            pltpu.VMEM((total, WIDE), jnp.bfloat16),
            pltpu.VMEM((5, total, 128), jnp.float32),
            pltpu.VMEM((5, total + na + nb, 128), jnp.float32),
            pltpu.SemaphoreType.DMA((len(pieces),)),
        ],
        cost_estimate=score_cost(total, vocab_rows),
    )(place, *pieces, near, head_weight)


def finish_kernel(me_ref, gathered, info, device, offsets, lengths, logprob, entropy, sequence):
    peaks = gathered[:, 0, :]
    sums = gathered[:, 1, :]
    top = jnp.max(peaks, axis=0, keepdims=True)
    shift_by = peaks - top
    factor = jnp.exp(shift_by)
    sum_exp = jnp.sum(factor * sums, axis=0, keepdims=True)
    spread = jnp.sum(factor * (gathered[:, 2, :] + shift_by * sums), axis=0, keepdims=True)
    target_logit = jnp.sum(gathered[:, 3, :], axis=0, keepdims=True)
    log_total = jnp.log(sum_exp)
    valid = info[5:6, :] > 0.5
    row_logprob = jnp.where(valid, target_logit - top - log_total, 0.0)
    row_entropy = jnp.where(valid, log_total - spread / sum_exp, 0.0)
    position = device[...] * ROWS + info[4:5, :].astype(jnp.int32)
    position = jnp.where(valid, position, -1)
    own = me_ref[0] * ROWS + lax.broadcasted_iota(jnp.int32, (ROWS, 1), 0)
    mine = position == own

    def across(column):
        count = column.shape[0]
        row = lax.broadcasted_iota(jnp.int32, (count, count), 0)
        lane = lax.broadcasted_iota(jnp.int32, (count, count), 1)
        return jnp.sum(jnp.where(row == lane, column, 0), axis=0, keepdims=True)

    def down(line):
        count = line.shape[1]
        row = lax.broadcasted_iota(jnp.int32, (count, count), 0)
        lane = lax.broadcasted_iota(jnp.int32, (count, count), 1)
        return jnp.sum(jnp.where(row == lane, line, 0), axis=1, keepdims=True)

    logprob[...] = across(jnp.sum(jnp.where(mine, row_logprob, 0.0), axis=1, keepdims=True))
    entropy[...] = across(jnp.sum(jnp.where(mine, row_entropy, 0.0), axis=1, keepdims=True))
    first = down(offsets[...])
    inside = (position >= first) & (position < first + down(lengths[...]))
    totals = jnp.sum(jnp.where(inside, row_logprob, 0.0), axis=1, keepdims=True)
    sequence[...] = across(totals) / lengths[...].astype(jnp.float32)


def finish(me, gathered, info, offsets, lengths):
    vmem = pl.BlockSpec(memory_space=pltpu.VMEM)
    count = lengths.shape[0]
    return pl.pallas_call(
        finish_kernel,
        name="finish",
        out_shape=(
            jax.ShapeDtypeStruct((1, ROWS), jnp.float32),
            jax.ShapeDtypeStruct((1, ROWS), jnp.float32),
            jax.ShapeDtypeStruct((1, count), jnp.float32),
        ),
        in_specs=[pl.BlockSpec(memory_space=pltpu.SMEM)] + [vmem] * 5,
        out_specs=(vmem, vmem, vmem),
    )(me[None], gathered, info, slot_devices()[None, :], offsets[None, :], lengths[None, :])


def slot_devices():
    device = np.zeros((64 * LIVE,), np.int32)
    for z in range(4):
        for y in range(4):
            for slot in range(LINE):
                at = (
                    z * 4 * ROWS_A + y * ROWS_A + slot
                    if slot < ROWS_A
                    else 16 * ROWS_A + y * 4 * ROWS_B + z * ROWS_B + slot - ROWS_A
                )
                device[at] = (slot // LIVE) * 16 + z * 4 + y
    return device


def local(hidden, norm_gain, head_weight, targets, lengths, offsets, loss_mask):
    me = lax.axis_index("tensor")
    x, z, y = me // 16, (me // 4) % 4, me % 4
    rows = pack(hidden, targets[None, :], loss_mask[None, :])
    line = [rows] + three_ahead(rows, X)
    part_a, part_b = prepare(x[None], norm_gain[None, :], line)
    row_a = [part_a] + three_ahead(part_a, Y)
    row_b = [part_b] + three_ahead(part_b, Z)
    own_a = jnp.concatenate(in_order(row_a, y), axis=0)
    own_b = jnp.concatenate(in_order(row_b, z), axis=0)
    up_a = from_ahead(own_a, Z, 1)
    down_a = from_ahead(own_a, Z, 3)
    up_b = from_ahead(own_b, Y, 1)
    down_b = from_ahead(own_b, Y, 3)
    na, nb = own_a.shape[0], own_b.shape[0]
    far_a = [from_ahead(up_a[: na // 2], Z, 1), from_ahead(down_a[na // 2 :], Z, 3)]
    far_b = [from_ahead(up_b[: nb // 2], Y, 1), from_ahead(down_b[nb // 2 :], Y, 3)]

    place = jnp.stack([me * head_weight.shape[0], z, y])
    near = score_near(place, [own_a, own_b], head_weight)
    stats, info = score_rest(
        place, [up_a, *far_a, down_a, up_b, *far_b, down_b], near, head_weight, na, nb
    )
    copies = jnp.broadcast_to(stats[None], (64,) + stats.shape)
    gathered = lax.all_to_all(copies, "tensor", 0, 0, tiled=True)
    token_logprob, token_entropy, score = finish(me, gathered, info, offsets, lengths)
    return token_logprob[0], token_entropy[0], score[0]


def solution(mesh):
    return jax.shard_map(
        local,
        mesh=mesh,
        in_specs=(
            P(("dp", "tensor"), None),
            P(),
            P(("dp", "tensor"), None),
            P(("dp", "tensor")),
            P("dp"),
            P("dp"),
            P(("dp", "tensor")),
        ),
        out_specs=(P(("dp", "tensor")), P(("dp", "tensor")), P("dp")),
        check_vma=False,
    )
```

profile of v0, /device:TPU:0, one launch (start us, length us, event | category | flops | bytes accessed | tf_op | source)
XLA Modules:
  0.0 115.1 jit_solution(7312315329541967010)
XLA Ops:
  0.6 1.7 %pack.1.rows0 = bf16[16,4224]{1,0:T(8,128)(2,1)} custom-call(bf16[16,4096]{1,0:T(8,128)(2,1)} %hidden_ref.1, s32[1,16]{1,0:T(1,128)} %bitcast.14, s32[1,16]{1,0:T(1,128)} %bitcast.15), custom_call_target="tpu_custom_call" | custom-call | flops 67584 | bytes 270336 | tf_op jit(solution)/shard_map/pack/pallas_call | solution.py:74
  2.3 1.6 %collective-permute-start.2 = (bf16[16,4224]{1,0:T(8,128)(2,1)}, bf16[16,4224]{1,0:T(8,128)(2,1)S(1)}, u32[]{:S(2)}, u32[]{:S(2)}) collective-permute-start(bf16[16,4224]{1,0:T(8,128)(2,1)} %pack.1.rows0), channel_id=1, source_target_pairs={{0,16},{1,17},{2,18},{3,19},{4,20},{5,21},{6,22},{7,23},{8,24},{9,... | collective-permute-start | bytes 405512 | tf_op jit(solution)/shard_map/ppermute | solution.py:37
  3.9 2.7 %collective-permute-start.1 = (bf16[16,4224]{1,0:T(8,128)(2,1)}, bf16[16,4224]{1,0:T(8,128)(2,1)S(1)}, u32[]{:S(2)}, u32[]{:S(2)}) collective-permute-start(bf16[16,4224]{1,0:T(8,128)(2,1)} %pack.1.rows0), channel_id=1, source_target_pairs={{0,32},{1,33},{2,34},{3,35},{4,36},{5,37},{6,38},{7,39},{8,40},{9,... | collective-permute-start | bytes 405512 | tf_op jit(solution)/shard_map/ppermute | solution.py:37
  6.6 1.4 %collective-permute-start = (bf16[16,4224]{1,0:T(8,128)(2,1)}, bf16[16,4224]{1,0:T(8,128)(2,1)S(1)}, u32[]{:S(2)}, u32[]{:S(2)}) collective-permute-start(bf16[16,4224]{1,0:T(8,128)(2,1)} %pack.1.rows0), channel_id=1, source_target_pairs={{0,48},{1,49},{2,50},{3,51},{4,52},{5,53},{6,54},{7,55},{8,56},{9,... | collective-permute-start | bytes 405512 | tf_op jit(solution)/shard_map/ppermute | solution.py:37
  8.1 0.9 collective-permute-done.2.rows3
  9.0 4.1 %collective-permute-done.1.rows2 = bf16[16,4224]{1,0:T(8,128)(2,1)S(1)} collective-permute-done((bf16[16,4224]{1,0:T(8,128)(2,1)}, bf16[16,4224]{1,0:T(8,128)(2,1)S(1)}, u32[]{:S(2)}, u32[]{:S(2)}) %collective-permute-start.1) | collective-permute-done | bytes 135200 | tf_op jit(solution)/shard_map/ppermute | solution.py:37
  13.7 2.3 %prepare.1 = (bf16[24,4224]{1,0:T(8,128)(2,1)}, bf16[16,4224]{1,0:T(8,128)(2,1)}) custom-call(s32[1]{0:T(128)} %bitcast.4.own_ref, f32[1,4096]{1,0:T(1,128)} %bitcast.13, bf16[16,4224]{1,0:T(8,128)(2,1)} %pack.1.rows0, bf16[16,4224]{1,0:T(8,128)(2,1)} %copy-done.6, bf16[16,4224]{1,0:T(8,128)(2,1)} %copy-done.5, bf16[16,4224]{1,0:T(8,128)(2,1)} %copy-done.4), custom_call_target="tpu_custom_call" | custom-call | flops 21626880 | bytes 878592 | tf_op jit(solution)/shard_map/prepare/pallas_call | solution.py:111
  16.0 1.9 %collective-permute-start.12 = (bf16[16,4224]{1,0:T(8,128)(2,1)}, bf16[16,4224]{1,0:T(8,128)(2,1)S(1)}, u32[]{:S(2)}, u32[]{:S(2)}) collective-permute-start(bf16[16,4224]{1,0:T(8,128)(2,1)} %get-tuple-element.11), channel_id=1, source_target_pairs={{0,4},{1,5},{2,6},{3,7},{4,8},{5,9},{6,10},{7,11},{8,12},{9,13},{1... | collective-permute-start | bytes 405512 | tf_op jit(solution)/shard_map/ppermute | solution.py:37
  18.0 3.6 %collective-permute-start.11 = (bf16[16,4224]{1,0:T(8,128)(2,1)}, bf16[16,4224]{1,0:T(8,128)(2,1)S(1)}, u32[]{:S(2)}, u32[]{:S(2)}) collective-permute-start(bf16[16,4224]{1,0:T(8,128)(2,1)} %get-tuple-element.11), channel_id=1, source_target_pairs={{0,8},{1,9},{2,10},{3,11},{4,12},{5,13},{6,14},{7,15},{8,0},{9,1},... | collective-permute-start | bytes 405512 | tf_op jit(solution)/shard_map/ppermute | solution.py:37
  21.5 1.0 collective-permute-start.10
  22.5 1.6 %collective-permute-start.5 = (bf16[24,4224]{1,0:T(8,128)(2,1)}, bf16[24,4224]{1,0:T(8,128)(2,1)S(1)}, u32[]{:S(2)}, u32[]{:S(2)}) collective-permute-start(bf16[24,4224]{1,0:T(8,128)(2,1)} %get-tuple-element.10), channel_id=1, source_target_pairs={{0,1},{1,2},{2,3},{3,0},{4,5},{5,6},{6,7},{7,4},{8,9},{9,10},{10,1... | collective-permute-start | bytes 608264 | tf_op jit(solution)/shard_map/ppermute | solution.py:37
  24.1 2.9 %collective-permute-start.4 = (bf16[24,4224]{1,0:T(8,128)(2,1)}, bf16[24,4224]{1,0:T(8,128)(2,1)S(1)}, u32[]{:S(2)}, u32[]{:S(2)}) collective-permute-start(bf16[24,4224]{1,0:T(8,128)(2,1)} %get-tuple-element.10), channel_id=1, source_target_pairs={{0,2},{1,3},{2,0},{3,1},{4,6},{5,7},{6,4},{7,5},{8,10},{9,11},{10,... | collective-permute-start | bytes 608264 | tf_op jit(solution)/shard_map/ppermute | solution.py:37
  27.0 1.3 %collective-permute-start.3 = (bf16[24,4224]{1,0:T(8,128)(2,1)}, bf16[24,4224]{1,0:T(8,128)(2,1)S(1)}, u32[]{:S(2)}, u32[]{:S(2)}) collective-permute-start(bf16[24,4224]{1,0:T(8,128)(2,1)} %get-tuple-element.10), channel_id=1, source_target_pairs={{0,3},{1,0},{2,1},{3,2},{4,7},{5,4},{6,5},{7,6},{8,11},{9,8},{10,9... | collective-permute-start | bytes 608264 | tf_op jit(solution)/shard_map/ppermute | solution.py:37
  28.4 1.0 select_select_fusion.7
  29.4 2.5 %collective-permute-done.5 = bf16[24,4224]{1,0:T(8,128)(2,1)S(1)} collective-permute-done((bf16[24,4224]{1,0:T(8,128)(2,1)}, bf16[24,4224]{1,0:T(8,128)(2,1)S(1)}, u32[]{:S(2)}, u32[]{:S(2)}) %collective-permute-start.5) | collective-permute-done | bytes 202784 | tf_op jit(solution)/shard_map/ppermute | solution.py:37
  31.9 2.8 %collective-permute-done.4 = bf16[24,4224]{1,0:T(8,128)(2,1)S(1)} collective-permute-done((bf16[24,4224]{1,0:T(8,128)(2,1)}, bf16[24,4224]{1,0:T(8,128)(2,1)S(1)}, u32[]{:S(2)}, u32[]{:S(2)}) %collective-permute-start.4) | collective-permute-done | bytes 202784 | tf_op jit(solution)/shard_map/ppermute | solution.py:37
  34.6 1.0 select_select_fusion.3
  35.7 1.1 collective-permute-start.8
  36.8 2.2 %collective-permute-start.6 = (bf16[96,4224]{1,0:T(8,128)(2,1)S(1)}, bf16[96,4224]{1,0:T(8,128)(2,1)S(1)}, u32[]{:S(2)}, u32[]{:S(2)}) collective-permute-start(bf16[96,4224]{1,0:T(8,128)(2,1)S(1)} %pad_maximum_fusion.refs_0_), channel_id=1, source_target_pairs={{0,12},{1,13},{2,14},{3,15},{4,0},{5,1},{6,2},{7,3},{8,4},{9,5},{1... | collective-permute-start | bytes 2433032 | tf_op jit(solution)/shard_map/ppermute | solution.py:37
  39.1 1.2 %collective-permute-start.15 = (bf16[64,4224]{1,0:T(8,128)(2,1)S(1)}, bf16[64,4224]{1,0:T(8,128)(2,1)}, u32[]{:S(2)}, u32[]{:S(2)}) collective-permute-start(bf16[64,4224]{1,0:T(8,128)(2,1)S(1)} %pad_maximum_fusion.1.refs_1_), channel_id=1, source_target_pairs={{0,1},{1,2},{2,3},{3,0},{4,5},{5,6},{6,7},{7,4},{8,9},{9,10},{10,1... | collective-permute-start | bytes 1622024 | tf_op jit(solution)/shard_map/ppermute | solution.py:37
  40.3 2.1 %collective-permute-start.13 = (bf16[64,4224]{1,0:T(8,128)(2,1)S(1)}, bf16[64,4224]{1,0:T(8,128)(2,1)}, u32[]{:S(2)}, u32[]{:S(2)}) collective-permute-start(bf16[64,4224]{1,0:T(8,128)(2,1)S(1)} %pad_maximum_fusion.1.refs_1_), channel_id=1, source_target_pairs={{0,3},{1,0},{2,1},{3,2},{4,7},{5,4},{6,5},{7,6},{8,11},{9,8},{10,9... | collective-permute-start | bytes 1622024 | tf_op jit(solution)/shard_map/ppermute | solution.py:37
  42.4 11.6 %collective-permute-done.8.refs_3_ = bf16[96,4224]{1,0:T(8,128)(2,1)S(1)} collective-permute-done((bf16[96,4224]{1,0:T(8,128)(2,1)S(1)}, bf16[96,4224]{1,0:T(8,128)(2,1)S(1)}, u32[]{:S(2)}, u32[]{:S(2)}) %collective-permute-start.8) | collective-permute-done | bytes 811040 | tf_op jit(solution)/shard_map/ppermute | solution.py:37
  54.5 0.9 copy-done.3
  55.4 3.0 %collective-permute-start.7 = (bf16[48,4224]{1,0:T(8,128)(2,1)S(1)}, bf16[48,4224]{1,0:T(8,128)(2,1)}, u32[]{:S(2)}, u32[]{:S(2)}) collective-permute-start(bf16[48,4224]{1,0:T(8,128)(2,1)S(1)} %slice.16), channel_id=1, source_target_pairs={{0,12},{1,13},{2,14},{3,15},{4,0},{5,1},{6,2},{7,3},{8,4},{9,5},{1... | collective-permute-start | bytes 1216520 | tf_op jit(solution)/shard_map/ppermute | solution.py:37
  58.3 1.0 slice.19
  59.3 3.2 %collective-permute-start.16 = (bf16[32,4224]{1,0:T(8,128)(2,1)S(1)}, bf16[32,4224]{1,0:T(8,128)(2,1)S(1)}, u32[]{:S(2)}, u32[]{:S(2)}) collective-permute-start(bf16[32,4224]{1,0:T(8,128)(2,1)S(1)} %slice.19), channel_id=1, source_target_pairs={{0,1},{1,2},{2,3},{3,0},{4,5},{5,6},{6,7},{7,4},{8,9},{9,10},{10,1... | collective-permute-start | bytes 811016 | tf_op jit(solution)/shard_map/ppermute | solution.py:37
  62.5 1.0 slice.18
  64.3 11.9 %near.1.refs_8_ = f32[5,160,128]{2,1,0:T(8,128)} custom-call(s32[3]{0:T(128)} %pad_add_fusion.place_ref, bf16[96,4224]{1,0:T(8,128)(2,1)} %copy-done, bf16[64,4224]{1,0:T(8,128)(2,1)} %copy-done.1, bf16[2004,4096]{1,0:T(8,128)(2,1)} %refs_9_.1), custom_call_target="tpu_custom_call" | custom-call | flops 2626682880 | bytes 17768448 | tf_op jit(solution)/shard_map/near/pallas_call | solution.py:244
  77.0 16.5 %rest.1 = (f32[4,640]{1,0:T(4,128)}, f32[8,640]{1,0:T(8,128)}) custom-call(s32[3]{0:T(128)} %pad_add_fusion.place_ref, bf16[96,4224]{1,0:T(8,128)(2,1)} %copy-done.3, bf16[48,4224]{1,0:T(8,128)(2,1)} %collective-permute-done.7.refs_1_, bf16[48,4224]{1,0:T(8,128)(2,1)} %collective-permute-done.9.refs_2_, bf16[96,4224]{1,0:T(8,128)(2,1)} %copy-done.2, ...), custom_call_target="tpu_custom_call" | custom-call | flops 7880048640 | bytes 20471808 | tf_op jit(solution)/shard_map/rest/pallas_call | solution.py:264
  93.5 0.8 broadcast_in_dim.32
  94.3 18.8 %all_to_all.5.gathered = f32[64,4,640]{2,1,0:T(4,128)} all-to-all(f32[64,4,640]{2,1,0:T(4,128)S(1)} %broadcast_in_dim.32), channel_id=1, replica_groups=mesh['dp'=2,'tensor'=64] {'tensor'}, dimensions={0} | all-to-all | bytes 1310720 | tf_op jit(solution)/shard_map/all_to_all | solution.py:381
  113.1 2.0 %finish.1 = (f32[1,16]{1,0:T(1,128)}, f32[1,16]{1,0:T(1,128)}, f32[1,12]{1,0:T(1,128)}) custom-call(s32[1]{0:T(128)} %bitcast.me_ref, f32[64,4,640]{2,1,0:T(4,128)} %all_to_all.5.gathered, f32[8,640]{1,0:T(8,128)} %get-tuple-element.13.info, s32[1,640]{1,0:T(1,128)} %constant.84.clone.device, s32[1,12]{1,0:T(1,128)} %bitcast.16, s32[1,12]{1,0:T(1,128)} %bitcast.17), custom_call_target="tpu_custom_call" | custom-call | tf_op jit(solution)/shard_map/finish/pallas_call | solution.py:330
  (36 shorter events, 2.9 us)
Async XLA Ops:
  2.3 6.7 %collective-permute-start.2 = (bf16[16,4224]{1,0:T(8,128)(2,1)}, bf16[16,4224]{1,0:T(8,128)(2,1)S(1)}, u32[]{:S(2)}, u32[]{:S(2)}) collective-permute-start(bf16[16,4224]{1,0:T(8,128)(2,1)} %pack.1.rows0), channel_id=1, source_target_pairs={{0,16},{1,17},{2,18},{3,19},{4,20},{5,21},{6,22},{7,23},{8,24},{9,... | collective-permute-start | bytes 405512 | tf_op jit(solution)/shard_map/ppermute | solution.py:37
  3.9 9.1 %collective-permute-start.1 = (bf16[16,4224]{1,0:T(8,128)(2,1)}, bf16[16,4224]{1,0:T(8,128)(2,1)S(1)}, u32[]{:S(2)}, u32[]{:S(2)}) collective-permute-start(bf16[16,4224]{1,0:T(8,128)(2,1)} %pack.1.rows0), channel_id=1, source_target_pairs={{0,32},{1,33},{2,34},{3,35},{4,36},{5,37},{6,38},{7,39},{8,40},{9,... | collective-permute-start | bytes 405512 | tf_op jit(solution)/shard_map/ppermute | solution.py:37
  6.6 6.4 %collective-permute-start = (bf16[16,4224]{1,0:T(8,128)(2,1)}, bf16[16,4224]{1,0:T(8,128)(2,1)S(1)}, u32[]{:S(2)}, u32[]{:S(2)}) collective-permute-start(bf16[16,4224]{1,0:T(8,128)(2,1)} %pack.1.rows0), channel_id=1, source_target_pairs={{0,48},{1,49},{2,50},{3,51},{4,52},{5,53},{6,54},{7,55},{8,56},{9,... | collective-permute-start | bytes 405512 | tf_op jit(solution)/shard_map/ppermute | solution.py:37
  9.0 4.1 %copy-start.4 = (bf16[16,4224]{1,0:T(8,128)(2,1)}, bf16[16,4224]{1,0:T(8,128)(2,1)S(1)}, u32[]{:S(2)}) copy-start(bf16[16,4224]{1,0:T(8,128)(2,1)S(1)} %collective-permute-done.2.rows3) | copy-start | bytes 405508
  13.0 0.7 copy-start.5
  13.0 0.7 copy-start.6
  16.0 11.0 %collective-permute-start.12 = (bf16[16,4224]{1,0:T(8,128)(2,1)}, bf16[16,4224]{1,0:T(8,128)(2,1)S(1)}, u32[]{:S(2)}, u32[]{:S(2)}) collective-permute-start(bf16[16,4224]{1,0:T(8,128)(2,1)} %get-tuple-element.11), channel_id=1, source_target_pairs={{0,4},{1,5},{2,6},{3,7},{4,8},{5,9},{6,10},{7,11},{8,12},{9,13},{1... | collective-permute-start | bytes 405512 | tf_op jit(solution)/shard_map/ppermute | solution.py:37
  18.0 10.4 %collective-permute-start.11 = (bf16[16,4224]{1,0:T(8,128)(2,1)}, bf16[16,4224]{1,0:T(8,128)(2,1)S(1)}, u32[]{:S(2)}, u32[]{:S(2)}) collective-permute-start(bf16[16,4224]{1,0:T(8,128)(2,1)} %get-tuple-element.11), channel_id=1, source_target_pairs={{0,8},{1,9},{2,10},{3,11},{4,12},{5,13},{6,14},{7,15},{8,0},{9,1},... | collective-permute-start | bytes 405512 | tf_op jit(solution)/shard_map/ppermute | solution.py:37
  21.5 6.8 %collective-permute-start.10 = (bf16[16,4224]{1,0:T(8,128)(2,1)}, bf16[16,4224]{1,0:T(8,128)(2,1)S(1)}, u32[]{:S(2)}, u32[]{:S(2)}) collective-permute-start(bf16[16,4224]{1,0:T(8,128)(2,1)} %get-tuple-element.11), channel_id=1, source_target_pairs={{0,12},{1,13},{2,14},{3,15},{4,0},{5,1},{6,2},{7,3},{8,4},{9,5},{1... | collective-permute-start | bytes 405512 | tf_op jit(solution)/shard_map/ppermute | solution.py:37
  22.5 9.3 %collective-permute-start.5 = (bf16[24,4224]{1,0:T(8,128)(2,1)}, bf16[24,4224]{1,0:T(8,128)(2,1)S(1)}, u32[]{:S(2)}, u32[]{:S(2)}) collective-permute-start(bf16[24,4224]{1,0:T(8,128)(2,1)} %get-tuple-element.10), channel_id=1, source_target_pairs={{0,1},{1,2},{2,3},{3,0},{4,5},{5,6},{6,7},{7,4},{8,9},{9,10},{10,1... | collective-permute-start | bytes 608264 | tf_op jit(solution)/shard_map/ppermute | solution.py:37
  24.1 10.5 %collective-permute-start.4 = (bf16[24,4224]{1,0:T(8,128)(2,1)}, bf16[24,4224]{1,0:T(8,128)(2,1)S(1)}, u32[]{:S(2)}, u32[]{:S(2)}) collective-permute-start(bf16[24,4224]{1,0:T(8,128)(2,1)} %get-tuple-element.10), channel_id=1, source_target_pairs={{0,2},{1,3},{2,0},{3,1},{4,6},{5,7},{6,4},{7,5},{8,10},{9,11},{10,... | collective-permute-start | bytes 608264 | tf_op jit(solution)/shard_map/ppermute | solution.py:37
  27.0 7.6 %collective-permute-start.3 = (bf16[24,4224]{1,0:T(8,128)(2,1)}, bf16[24,4224]{1,0:T(8,128)(2,1)S(1)}, u32[]{:S(2)}, u32[]{:S(2)}) collective-permute-start(bf16[24,4224]{1,0:T(8,128)(2,1)} %get-tuple-element.10), channel_id=1, source_target_pairs={{0,3},{1,0},{2,1},{3,2},{4,7},{5,4},{6,5},{7,6},{8,11},{9,8},{10,9... | collective-permute-start | bytes 608264 | tf_op jit(solution)/shard_map/ppermute | solution.py:37
  35.7 23.6 %copy-start = (bf16[96,4224]{1,0:T(8,128)(2,1)}, bf16[96,4224]{1,0:T(8,128)(2,1)S(1)}, u32[]{:S(2)}) copy-start(bf16[96,4224]{1,0:T(8,128)(2,1)S(1)} %pad_maximum_fusion.refs_0_) | copy-start | bytes 2433028
  35.7 18.2 %collective-permute-start.8 = (bf16[96,4224]{1,0:T(8,128)(2,1)S(1)}, bf16[96,4224]{1,0:T(8,128)(2,1)S(1)}, u32[]{:S(2)}, u32[]{:S(2)}) collective-permute-start(bf16[96,4224]{1,0:T(8,128)(2,1)S(1)} %pad_maximum_fusion.refs_0_), channel_id=1, source_target_pairs={{0,4},{1,5},{2,6},{3,7},{4,8},{5,9},{6,10},{7,11},{8,12},{9,13},{1... | collective-permute-start | bytes 2433032 | tf_op jit(solution)/shard_map/ppermute | solution.py:37
  36.8 17.6 %collective-permute-start.6 = (bf16[96,4224]{1,0:T(8,128)(2,1)S(1)}, bf16[96,4224]{1,0:T(8,128)(2,1)S(1)}, u32[]{:S(2)}, u32[]{:S(2)}) collective-permute-start(bf16[96,4224]{1,0:T(8,128)(2,1)S(1)} %pad_maximum_fusion.refs_0_), channel_id=1, source_target_pairs={{0,12},{1,13},{2,14},{3,15},{4,0},{5,1},{6,2},{7,3},{8,4},{9,5},{1... | collective-permute-start | bytes 2433032 | tf_op jit(solution)/shard_map/ppermute | solution.py:37
  39.1 25.2 %copy-start.1 = (bf16[64,4224]{1,0:T(8,128)(2,1)}, bf16[64,4224]{1,0:T(8,128)(2,1)S(1)}, u32[]{:S(2)}) copy-start(bf16[64,4224]{1,0:T(8,128)(2,1)S(1)} %pad_maximum_fusion.1.refs_1_) | copy-start | bytes 1622020
  39.1 19.2 %collective-permute-start.15 = (bf16[64,4224]{1,0:T(8,128)(2,1)S(1)}, bf16[64,4224]{1,0:T(8,128)(2,1)}, u32[]{:S(2)}, u32[]{:S(2)}) collective-permute-start(bf16[64,4224]{1,0:T(8,128)(2,1)S(1)} %pad_maximum_fusion.1.refs_1_), channel_id=1, source_target_pairs={{0,1},{1,2},{2,3},{3,0},{4,5},{5,6},{6,7},{7,4},{8,9},{9,10},{10,1... | collective-permute-start | bytes 1622024 | tf_op jit(solution)/shard_map/ppermute | solution.py:37
  40.3 22.2 %collective-permute-start.13 = (bf16[64,4224]{1,0:T(8,128)(2,1)S(1)}, bf16[64,4224]{1,0:T(8,128)(2,1)}, u32[]{:S(2)}, u32[]{:S(2)}) collective-permute-start(bf16[64,4224]{1,0:T(8,128)(2,1)S(1)} %pad_maximum_fusion.1.refs_1_), channel_id=1, source_target_pairs={{0,3},{1,0},{2,1},{3,2},{4,7},{5,4},{6,5},{7,6},{8,11},{9,8},{10,9... | collective-permute-start | bytes 1622024 | tf_op jit(solution)/shard_map/ppermute | solution.py:37
  54.0 22.2 %copy-start.2 = (bf16[96,4224]{1,0:T(8,128)(2,1)}, bf16[96,4224]{1,0:T(8,128)(2,1)S(1)}, u32[]{:S(2)}) copy-start(bf16[96,4224]{1,0:T(8,128)(2,1)S(1)} %collective-permute-done.8.refs_3_) | copy-start | bytes 2433028
  54.0 22.3 %collective-permute-start.9 = (bf16[48,4224]{1,0:T(8,128)(2,1)S(1)}, bf16[48,4224]{1,0:T(8,128)(2,1)}, u32[]{:S(2)}, u32[]{:S(2)}) collective-permute-start(bf16[48,4224]{1,0:T(8,128)(2,1)S(1)} %slice.17), channel_id=1, source_target_pairs={{0,4},{1,5},{2,6},{3,7},{4,8},{5,9},{6,10},{7,11},{8,12},{9,13},{1... | collective-permute-start | bytes 1216520 | tf_op jit(solution)/shard_map/ppermute | solution.py:37
  54.4 0.9 copy-start.3
  55.4 20.9 %collective-permute-start.7 = (bf16[48,4224]{1,0:T(8,128)(2,1)S(1)}, bf16[48,4224]{1,0:T(8,128)(2,1)}, u32[]{:S(2)}, u32[]{:S(2)}) collective-permute-start(bf16[48,4224]{1,0:T(8,128)(2,1)S(1)} %slice.16), channel_id=1, source_target_pairs={{0,12},{1,13},{2,14},{3,15},{4,0},{5,1},{6,2},{7,3},{8,4},{9,5},{1... | collective-permute-start | bytes 1216520 | tf_op jit(solution)/shard_map/ppermute | solution.py:37
  59.3 16.9 %collective-permute-start.16 = (bf16[32,4224]{1,0:T(8,128)(2,1)S(1)}, bf16[32,4224]{1,0:T(8,128)(2,1)S(1)}, u32[]{:S(2)}, u32[]{:S(2)}) collective-permute-start(bf16[32,4224]{1,0:T(8,128)(2,1)S(1)} %slice.19), channel_id=1, source_target_pairs={{0,1},{1,2},{2,3},{3,0},{4,5},{5,6},{6,7},{7,4},{8,9},{9,10},{10,1... | collective-permute-start | bytes 811016 | tf_op jit(solution)/shard_map/ppermute | solution.py:37
  63.5 12.8 %collective-permute-start.14 = (bf16[32,4224]{1,0:T(8,128)(2,1)S(1)}, bf16[32,4224]{1,0:T(8,128)(2,1)S(1)}, u32[]{:S(2)}, u32[]{:S(2)}) collective-permute-start(bf16[32,4224]{1,0:T(8,128)(2,1)S(1)} %slice.18), channel_id=1, source_target_pairs={{0,3},{1,0},{2,1},{3,2},{4,7},{5,4},{6,5},{7,6},{8,11},{9,8},{10,9... | collective-permute-start | bytes 811016 | tf_op jit(solution)/shard_map/ppermute | solution.py:37
  76.2 0.7 copy-start.7
  76.3 0.8 copy-start.8
where the time goes:
time: 116 us; the launch traced here: 115 us
  Pallas kernels  34.3 us (30%)
  starting transfers between devices  31.4 us (27%)
  waiting for transfers between devices  21.8 us (19%)
  blocking collectives  18.8 us (16%)
  local copies, waits for them, and re-layouts  5.15 us (4%)
  other arithmetic  2.79 us (2%)
    ppermute x17, starting transfers between devices, from_ahead(): return lax.ppermute(value, 'tensor', shifted_pairs(axis, step))  31.4 us
    ppermute x17, waiting for transfers between devices, from_ahead(): return lax.ppermute(value, 'tensor', shifted_pairs(axis, step))  21.8 us
    all_to_all x1, blocking collectives, local(): gathered = lax.all_to_all(copies, 'tensor', 0, 0, tiled=True)  18.8 us
    pallas_call x1, Pallas kernels, score_rest(): pl.pallas_call(functools.partial(rest_kernel, vocab_rows, len(pieces), na...  16.5 us
    pallas_call x1, Pallas kernels, score_near(): pl.pallas_call(functools.partial(near_kernel, vocab_rows, len(pieces)), n...  11.9 us
    unnamed x18, local copies, waits for them, and re-layouts  2.36 us
  transfers between devices with their start and end apart: 17, of which 5 were waited for; matrix products, arithmetic and copies ran while one was open for 3% of the time, Pallas kernels for 10%

commit v1 on v0

--- a/solution.py
+++ b/solution.py
@@ -41,8 +41,8 @@
     return [from_ahead(value, axis, 1), from_ahead(value, axis, 2), from_ahead(value, axis, 3)]
 
 
-def in_order(pieces, own):
-    return [lax.select_n((j - own) % 4, *pieces) for j in range(4)]
+def in_vmem(value):
+    return pltpu.with_memory_space_constraint(value, pltpu.VMEM)
 
 
 def pack_kernel(hidden_ref, targets_ref, mask_ref, out_ref):
@@ -81,6 +81,27 @@
             flops=ROWS * WIDE, bytes_accessed=4 * ROWS * WIDE, transcendentals=0
         ),
     )(hidden, targets, mask)
+
+
+def hold_kernel(weight_ref, out_ref, sem):
+    copy = pltpu.make_async_copy(weight_ref, out_ref, sem)
+    copy.start()
+    copy.wait()
+
+
+def hold(head_weight):
+    return pl.pallas_call(
+        hold_kernel,
+        name="hold",
+        out_shape=pltpu.VMEM(head_weight.shape, head_weight.dtype),
+        in_specs=[pl.BlockSpec(memory_space=pl.ANY)],
+        out_specs=pl.BlockSpec(memory_space=pltpu.VMEM),
+        scratch_shapes=[pltpu.SemaphoreType.DMA],
+        compiler_params=pltpu.CompilerParams(vmem_limit_bytes=4 * 1024 * 1024),
+        cost_estimate=pl.CostEstimate(
+            flops=0, bytes_accessed=2 * head_weight.size, transcendentals=0
+        ),
+    )(pltpu.with_memory_space_constraint(head_weight, pltpu.HBM))
 
 
 def prepare_kernel(own_ref, gain_ref, rows0, rows1, rows2, rows3, a_ref, b_ref):
@@ -117,6 +138,7 @@
         ),
         in_specs=[pl.BlockSpec(memory_space=pltpu.SMEM)] + [vmem] * 5,
         out_specs=(vmem, vmem),
+        compiler_params=pltpu.CompilerParams(vmem_limit_bytes=8 * 1024 * 1024),
         cost_estimate=pl.CostEstimate(
             flops=2 * 64 * LINE * WIDE, bytes_accessed=104 * WIDE * 2, transcendentals=64
         ),
@@ -191,7 +213,7 @@
 
 
 def rest_kernel(vocab_rows, n_pieces, na, nb, place_ref, *refs):
-    near_ref, weight_ref, out_ref, info_ref, held, acc, all_rows, sems = refs[n_pieces:]
+    near_ref, side_ref, weight_ref, out_ref, info_ref, held, acc, all_rows, sems = refs[n_pieces:]
     step = pl.program_id(0)
 
     @pl.when(step == 0)
@@ -204,15 +226,17 @@
     def _():
         z, y = place_ref[1], place_ref[2]
         for k in range(4):
-            to_a = pl.multiple_of(lax.rem(z + k, 4) * na, na)
-            to_b = pl.multiple_of(4 * na + lax.rem(y + k, 4) * nb, nb)
-            if k == 0:
-                all_rows[:, pl.ds(to_a, na), :] = near_ref[:, :na, :]
-                all_rows[:, pl.ds(to_b, nb), :] = near_ref[:, na:, :]
-            else:
-                at_a, at_b = (k - 1) * na, 3 * na + (k - 1) * nb
-                all_rows[:, pl.ds(to_a, na), :] = acc[:, at_a : at_a + na, :]
-                all_rows[:, pl.ds(to_b, nb), :] = acc[:, at_b : at_b + nb, :]
+            from_a, at_a = ((near_ref, 0), (side_ref, 0), (acc, 0), (side_ref, na))[k]
+            from_b, at_b = (near_ref, na) if k == 0 else (acc, na + (k - 1) * nb)
+            for j in range(4):
+                to_a = lax.rem(z + k, 4) * na + lax.rem(y + j, 4) * ROWS_A
+                to_b = 4 * na + lax.rem(y + k, 4) * nb + lax.rem(z + j, 4) * ROWS_B
+                one_a = slice(at_a + j * ROWS_A, at_a + (j + 1) * ROWS_A)
+                one_b = slice(at_b + j * ROWS_B, at_b + (j + 1) * ROWS_B)
+                into_a = pl.ds(pl.multiple_of(to_a, 8), ROWS_A)
+                into_b = pl.ds(pl.multiple_of(to_b, 8), ROWS_B)
+                all_rows[:, into_a, :] = from_a[:, one_a, :]
+                all_rows[:, into_b, :] = from_b[:, one_b, :]
         for at in range(0, all_rows.shape[1], 128):
             peaks, sums, spreads, picks, extra = [
                 all_rows[plane, at : at + 128, :].T for plane in range(5)
@@ -230,6 +254,10 @@
             info_ref[:, here] = extra[:8]
 
 
+def score_params():
+    return pltpu.CompilerParams(vmem_limit_bytes=24 * 1024 * 1024)
+
+
 def score_cost(total, vocab_rows):
     return pl.CostEstimate(
         flops=2 * total * vocab_rows * D,
@@ -238,12 +266,11 @@
     )
 
 
-def score_near(place, pieces, head_weight):
+def score_part(place, pieces, head_weight):
     total = sum(piece.shape[0] for piece in pieces)
     vocab_rows = head_weight.shape[0]
     return pl.pallas_call(
         functools.partial(near_kernel, vocab_rows, len(pieces)),
-        name="near",
         grid=(pl.cdiv(vocab_rows, VOCAB_TILE),),
         out_shape=jax.ShapeDtypeStruct((5, total, 128), jnp.float32),
         in_specs=[pl.BlockSpec(memory_space=pltpu.SMEM)]
@@ -254,36 +281,43 @@
             pltpu.VMEM((total, WIDE), jnp.bfloat16),
             pltpu.SemaphoreType.DMA((len(pieces),)),
         ],
+        compiler_params=score_params(),
         cost_estimate=score_cost(total, vocab_rows),
     )(place, *pieces, head_weight)
 
 
-def score_rest(place, pieces, near, head_weight, na, nb):
+def score_rest(place, pieces, near, side, head_weight, na, nb):
     total = sum(piece.shape[0] for piece in pieces)
+    slots = 4 * (na + nb)
     vocab_rows = head_weight.shape[0]
     return pl.pallas_call(
         functools.partial(rest_kernel, vocab_rows, len(pieces), na, nb),
         name="rest",
         grid=(pl.cdiv(vocab_rows, VOCAB_TILE),),
         out_shape=(
-            jax.ShapeDtypeStruct((4, total + na + nb), jnp.float32),
-            jax.ShapeDtypeStruct((8, total + na + nb), jnp.float32),
+            jax.ShapeDtypeStruct((4, slots), jnp.float32),
+            jax.ShapeDtypeStruct((8, slots), jnp.float32),
         ),
         in_specs=[pl.BlockSpec(memory_space=pltpu.SMEM)]
         + [pl.BlockSpec(memory_space=pl.ANY)] * len(pieces)
-        + [pl.BlockSpec(near.shape, lambda i: (0, 0, 0)), pl.BlockSpec((VOCAB_TILE, D), lambda i: (i, 0))],
+        + [
+            pl.BlockSpec(near.shape, lambda i: (0, 0, 0)),
+            pl.BlockSpec(side.shape, lambda i: (0, 0, 0)),
+            pl.BlockSpec((VOCAB_TILE, D), lambda i: (i, 0)),
+        ],
         out_specs=(
-            pl.BlockSpec((4, total + na + nb), lambda i: (0, 0)),
-            pl.BlockSpec((8, total + na + nb), lambda i: (0, 0)),
+            pl.BlockSpec((4, slots), lambda i: (0, 0)),
+            pl.BlockSpec((8, slots), lambda i: (0, 0)),
         ),
         scratch_shapes=[
             pltpu.VMEM((total, WIDE), jnp.bfloat16),
             pltpu.VMEM((5, total, 128), jnp.float32),
-            pltpu.VMEM((5, total + na + nb, 128), jnp.float32),
+            pltpu.VMEM((5, slots, 128), jnp.float32),
             pltpu.SemaphoreType.DMA((len(pieces),)),
         ],
+        compiler_params=score_params(),
         cost_estimate=score_cost(total, vocab_rows),
-    )(place, *pieces, near, head_weight)
+    )(place, *pieces, near, side, head_weight)
 
 
 def finish_kernel(me_ref, gathered, info, device, offsets, lengths, logprob, entropy, sequence):
@@ -330,6 +364,7 @@
     return pl.pallas_call(
         finish_kernel,
         name="finish",
+        compiler_params=pltpu.CompilerParams(vmem_limit_bytes=16 * 1024 * 1024),
         out_shape=(
             jax.ShapeDtypeStruct((1, ROWS), jnp.float32),
             jax.ShapeDtypeStruct((1, ROWS), jnp.float32),
@@ -359,23 +394,27 @@
     x, z, y = me // 16, (me // 4) % 4, me % 4
     rows = pack(hidden, targets[None, :], loss_mask[None, :])
     line = [rows] + three_ahead(rows, X)
-    part_a, part_b = prepare(x[None], norm_gain[None, :], line)
+    part_a, part_b = prepare(x[None], norm_gain[None, :], line[:1] + [in_vmem(item) for item in line[1:]])
     row_a = [part_a] + three_ahead(part_a, Y)
     row_b = [part_b] + three_ahead(part_b, Z)
-    own_a = jnp.concatenate(in_order(row_a, y), axis=0)
-    own_b = jnp.concatenate(in_order(row_b, z), axis=0)
+    own_a = jnp.concatenate(row_a, axis=0)
+    own_b = jnp.concatenate(row_b, axis=0)
     up_a = from_ahead(own_a, Z, 1)
     down_a = from_ahead(own_a, Z, 3)
     up_b = from_ahead(own_b, Y, 1)
     down_b = from_ahead(own_b, Y, 3)
     na, nb = own_a.shape[0], own_b.shape[0]
     far_a = [from_ahead(up_a[: na // 2], Z, 1), from_ahead(down_a[na // 2 :], Z, 3)]
+    far_a = [in_vmem(item) for item in far_a]
     far_b = [from_ahead(up_b[: nb // 2], Y, 1), from_ahead(down_b[nb // 2 :], Y, 3)]
+    far_b = [in_vmem(item) for item in far_b]
 
     place = jnp.stack([me * head_weight.shape[0], z, y])
-    near = score_near(place, [own_a, own_b], head_weight)
+    held_weight = hold(head_weight)
+    near = score_part(place, [own_a, own_b], held_weight)
+    side = score_part(place, [up_a, down_a], held_weight)
     stats, info = score_rest(
-        place, [up_a, *far_a, down_a, up_b, *far_b, down_b], near, head_weight, na, nb
+        place, [*far_a, in_vmem(up_b), *far_b, in_vmem(down_b)], near, side, held_weight, na, nb
     )
     copies = jnp.broadcast_to(stats[None], (64,) + stats.shape)
     gathered = lax.all_to_all(copies, "tensor", 0, 0, tiled=True)

time: 116 us -> 111 us (0.957)
  local copies, waits for them, and re-layouts: 5.15 us -> 15.9 us
  starting transfers between devices: 31.4 us -> 24.6 us
  waiting for transfers between devices: 21.8 us -> 16.9 us
  other arithmetic: 2.79 us -> 0.08 us
  Pallas kernels: 34.3 us -> 33 us
    unnamed x18 -> x20, local copies, waits for them, and re-layouts: 2.36 us -> 15 us
    pallas_call x2 -> x4, Pallas kernels: 13.9 us -> 22.4 us  [the longest x2 15.8 us: score_part(): pl.pallas_call(functools.partial(near_kernel, vocab_rows, len(pieces)), g...]
    pallas_call x1, Pallas kernels: 16.5 us -> 8.49 us  [score_rest(): pl.pallas_call(functools.partial(rest_kernel, vocab_rows, len(pieces), na...]
    ppermute x17, starting transfers between devices: 31.4 us -> 24.6 us  [from_ahead(): return lax.ppermute(value, 'tensor', shifted_pairs(axis, step))]
    ppermute x17, waiting for transfers between devices: 21.8 us -> 16.9 us  [from_ahead(): return lax.ppermute(value, 'tensor', shifted_pairs(axis, step))]
    select_n x2 -> x0, other arithmetic: 2.03 us -> none  [in_order(): return [lax.select_n((j - own) % 4, *pieces) for j in range(4)]]
    pallas_call x1, Pallas kernels: 2.3 us -> 0.45 us  [prepare(): pl.pallas_call(prepare_kernel, name='prepare', out_shape=(jax.ShapeDtypeS...]
  transfers between devices with their start and end apart: 17 -> 17, of which waited for: 5 -> 7; matrix products, arithmetic and copies ran while one was open for 3% -> 3% of each run, Pallas kernels for 10% -> 19%
where the time goes in v1:
time: 111 us; the launch traced here: 110 us
  Pallas kernels  33 us (30%)
  starting transfers between devices  24.6 us (22%)
  blocking collectives  19.2 us (17%)
  waiting for transfers between devices  16.9 us (15%)
  local copies, waits for them, and re-layouts  15.9 us (14%)
    ppermute x17, starting transfers between devices, from_ahead(): return lax.ppermute(value, 'tensor', shifted_pairs(axis, step))  24.6 us
    all_to_all x1, blocking collectives, local(): gathered = lax.all_to_all(copies, 'tensor', 0, 0, tiled=True)  19.2 us
    ppermute x17, waiting for transfers between devices, from_ahead(): return lax.ppermute(value, 'tensor', shifted_pairs(axis, step))  16.9 us
    pallas_call x2, Pallas kernels, score_part(): pl.pallas_call(functools.partial(near_kernel, vocab_rows, len(pieces)), g...  15.8 us
    unnamed x20, local copies, waits for them, and re-layouts  15 us
    pallas_call x1, Pallas kernels, score_rest(): pl.pallas_call(functools.partial(rest_kernel, vocab_rows, len(pieces), na...  8.49 us
    pallas_call x1, Pallas kernels, hold(): pl.pallas_call(hold_kernel, name='hold', out_shape=pltpu.VMEM(head_weight...  5.68 us
  transfers between devices with their start and end apart: 17, of which 7 were waited for; matrix products, arithmetic and copies ran while one was open for 3% of the time, Pallas kernels for 19%

profile of v1, /device:TPU:0, one launch (start us, length us, event | category | flops | bytes accessed | tf_op | source)
XLA Modules:
  0.0 110.5 jit_solution(1497280286102659619)
XLA Ops:
  0.6 1.7 %pack.1.rows0 = bf16[16,4224]{1,0:T(8,128)(2,1)} custom-call(bf16[16,4096]{1,0:T(8,128)(2,1)} %hidden_ref.1, s32[1,16]{1,0:T(1,128)} %bitcast.16, s32[1,16]{1,0:T(1,128)} %bitcast.17), custom_call_target="tpu_custom_call" | custom-call | flops 67584 | bytes 270336 | tf_op jit(solution)/shard_map/pack/pallas_call | solution.py:74
  2.3 2.9 %collective-permute-start = (bf16[16,4224]{1,0:T(8,128)(2,1)}, bf16[16,4224]{1,0:T(8,128)(2,1)S(1)}, u32[]{:S(2)}, u32[]{:S(2)}) collective-permute-start(bf16[16,4224]{1,0:T(8,128)(2,1)} %pack.1.rows0), channel_id=1, source_target_pairs={{0,48},{1,49},{2,50},{3,51},{4,52},{5,53},{6,54},{7,55},{8,56},{9,... | collective-permute-start | bytes 405512 | tf_op jit(solution)/shard_map/ppermute | solution.py:37
  5.2 0.8 collective-permute-start.1
  6.0 0.9 collective-permute-start.2
  6.9 4.4 %collective-permute-done.rows1 = bf16[16,4224]{1,0:T(8,128)(2,1)S(1)} collective-permute-done((bf16[16,4224]{1,0:T(8,128)(2,1)}, bf16[16,4224]{1,0:T(8,128)(2,1)S(1)}, u32[]{:S(2)}, u32[]{:S(2)}) %collective-permute-start) | collective-permute-done | bytes 135200 | tf_op jit(solution)/shard_map/ppermute | solution.py:37
  11.2 2.1 %collective-permute-done.1.rows2 = bf16[16,4224]{1,0:T(8,128)(2,1)S(1)} collective-permute-done((bf16[16,4224]{1,0:T(8,128)(2,1)}, bf16[16,4224]{1,0:T(8,128)(2,1)S(1)}, u32[]{:S(2)}, u32[]{:S(2)}) %collective-permute-start.1) | collective-permute-done | bytes 135200 | tf_op jit(solution)/shard_map/ppermute | solution.py:37
  13.3 1.5 %collective-permute-done.2.rows3 = bf16[16,4224]{1,0:T(8,128)(2,1)S(1)} collective-permute-done((bf16[16,4224]{1,0:T(8,128)(2,1)}, bf16[16,4224]{1,0:T(8,128)(2,1)S(1)}, u32[]{:S(2)}, u32[]{:S(2)}) %collective-permute-start.2) | collective-permute-done | bytes 135200 | tf_op jit(solution)/shard_map/ppermute | solution.py:37
  14.8 0.9 copy-done.2
  15.7 0.7 copy-done.3
  16.9 3.1 %collective-permute-start.3 = (bf16[24,4224]{1,0:T(8,128)(2,1)S(1)}, bf16[24,4224]{1,0:T(8,128)(2,1)S(1)}, u32[]{:S(2)}, u32[]{:S(2)}) collective-permute-start(bf16[24,4224]{1,0:T(8,128)(2,1)S(1)} %get-tuple-element.10), channel_id=1, source_target_pairs={{0,3},{1,0},{2,1},{3,2},{4,7},{5,4},{6,5},{7,6},{8,11},{9,8},{10,9... | collective-permute-start | bytes 608264 | tf_op jit(solution)/shard_map/ppermute | solution.py:37
  20.7 1.0 collective-permute-start.5
  21.6 4.0 %collective-permute-start.10 = (bf16[16,4224]{1,0:T(8,128)(2,1)S(1)}, bf16[16,4224]{1,0:T(8,128)(2,1)S(1)}, u32[]{:S(2)}, u32[]{:S(2)}) collective-permute-start(bf16[16,4224]{1,0:T(8,128)(2,1)S(1)} %get-tuple-element.11), channel_id=1, source_target_pairs={{0,12},{1,13},{2,14},{3,15},{4,0},{5,1},{6,2},{7,3},{8,4},{9,5},{1... | collective-permute-start | bytes 405512 | tf_op jit(solution)/shard_map/ppermute | solution.py:37
  25.7 0.7 constant_dynamic-update-slice_fusion.7
  26.3 4.3 %collective-permute-done.10 = bf16[16,4224]{1,0:T(8,128)(2,1)S(1)} collective-permute-done((bf16[16,4224]{1,0:T(8,128)(2,1)S(1)}, bf16[16,4224]{1,0:T(8,128)(2,1)S(1)}, u32[]{:S(2)}, u32[]{:S(2)}) %collective-permute-start.10) | collective-permute-done | bytes 135200 | tf_op jit(solution)/shard_map/ppermute | solution.py:37
  31.3 1.5 %collective-permute-done.11 = bf16[16,4224]{1,0:T(8,128)(2,1)S(1)} collective-permute-done((bf16[16,4224]{1,0:T(8,128)(2,1)S(1)}, bf16[16,4224]{1,0:T(8,128)(2,1)S(1)}, u32[]{:S(2)}, u32[]{:S(2)}) %collective-permute-start.11) | collective-permute-done | bytes 135200 | tf_op jit(solution)/shard_map/ppermute | solution.py:37
  32.9 0.7 constant_dynamic-update-slice_fusion.5
  33.6 2.9 %collective-permute-start.6 = (bf16[96,4224]{1,0:T(8,128)(2,1)S(1)}, bf16[96,4224]{1,0:T(8,128)(2,1)S(1)}, u32[]{:S(2)}, u32[]{:S(2)}) collective-permute-start(bf16[96,4224]{1,0:T(8,128)(2,1)S(1)} %constant_dynamic-update-slice_fusion.refs_0_), channel_id=1, source_target_pairs={{0,12},{1,13},{2,14},{3,15},{4,0},{5,1},{6,2},{7,3},{8,4},{9,5},{1... | collective-permute-start | bytes 2433032 | tf_op jit(solution)/shard_map/ppermute | solution.py:37
  36.6 0.7 collective-permute-done.12
  37.3 0.7 constant_dynamic-update-slice_fusion.4.refs_1_
  38.0 2.3 %collective-permute-start.13 = (bf16[64,4224]{1,0:T(8,128)(2,1)}, bf16[64,4224]{1,0:T(8,128)(2,1)S(1)}, u32[]{:S(2)}, u32[]{:S(2)}) collective-permute-start(bf16[64,4224]{1,0:T(8,128)(2,1)} %constant_dynamic-update-slice_fusion.4.refs_1_), channel_id=1, source_target_pairs={{0,3},{1,0},{2,1},{3,2},{4,7},{5,4},{6,5},{7,6},{8,11},{9,8},{10,9... | collective-permute-start | bytes 1622024 | tf_op jit(solution)/shard_map/ppermute | solution.py:37
  40.3 5.7 %hold.1.refs_2_.refs_8_ = bf16[2004,4096]{1,0:T(8,128)(2,1)S(1)} custom-call(bf16[2004,4096]{1,0:T(8,128)(2,1)} %weight_ref.1), custom_call_target="tpu_custom_call" | custom-call | bytes 16416768 | tf_op jit(solution)/shard_map/hold/pallas_call | solution.py:93
  46.0 5.6 %copy-done = bf16[2004,4096]{1,0:T(8,128)(2,1)} copy-done((bf16[2004,4096]{1,0:T(8,128)(2,1)}, bf16[2004,4096]{1,0:T(8,128)(2,1)S(1)}, u32[]{:S(2)}) %copy-start) | copy-done | bytes 16416792
  51.7 2.3 %collective-permute-done.6.refs_0_ = bf16[96,4224]{1,0:T(8,128)(2,1)S(1)} collective-permute-done((bf16[96,4224]{1,0:T(8,128)(2,1)S(1)}, bf16[96,4224]{1,0:T(8,128)(2,1)S(1)}, u32[]{:S(2)}, u32[]{:S(2)}) %collective-permute-start.6) | collective-permute-done | bytes 811040 | tf_op jit(solution)/shard_map/ppermute | solution.py:37
  54.1 3.8 %collective-permute-start.7 = (bf16[48,4224]{1,0:T(8,128)(2,1)S(1)}, bf16[48,4224]{1,0:T(8,128)(2,1)S(1)}, u32[]{:S(2)}, u32[]{:S(2)}) collective-permute-start(bf16[48,4224]{1,0:T(8,128)(2,1)S(1)} %slice.16), channel_id=1, source_target_pairs={{0,12},{1,13},{2,14},{3,15},{4,0},{5,1},{6,2},{7,3},{8,4},{9,5},{1... | collective-permute-start | bytes 1216520 | tf_op jit(solution)/shard_map/ppermute | solution.py:37
  58.0 5.7 %copy-done.1 = bf16[2004,4096]{1,0:T(8,128)(2,1)S(1)} copy-done((bf16[2004,4096]{1,0:T(8,128)(2,1)S(1)}, bf16[2004,4096]{1,0:T(8,128)(2,1)}, u32[]{:S(2)}) %copy-start.1) | copy-done | bytes 16416792
  63.7 8.4 %shard_map.103.refs_6_ = f32[5,160,128]{2,1,0:T(8,128)S(1)} custom-call(s32[3]{0:T(128)S(1)} %pad_add_fusion.place_ref, bf16[96,4224]{1,0:T(8,128)(2,1)S(1)} %constant_dynamic-update-slice_fusion.refs_0_, bf16[64,4224]{1,0:T(8,128)(2,1)} %constant_dynamic-update-slice_fusion.4.refs_1_, bf16[2004,4096]{1,0:T(8,128)(2,1)S(1)} %copy-done.1), custom_call_target="tpu_custom_call" | custom-call | flops 2626682880 | bytes 17768448 | tf_op jit(solution)/shard_map/pallas_call | solution.py:272
  72.1 0.7 collective-permute-start.14
  72.8 1.5 %collective-permute-start.16 = (bf16[32,4224]{1,0:T(8,128)(2,1)S(1)}, bf16[32,4224]{1,0:T(8,128)(2,1)S(1)}, u32[]{:S(2)}, u32[]{:S(2)}) collective-permute-start(bf16[32,4224]{1,0:T(8,128)(2,1)S(1)} %slice.19), channel_id=1, source_target_pairs={{0,1},{1,2},{2,3},{3,0},{4,5},{5,6},{6,7},{7,4},{8,9},{9,10},{10,1... | collective-permute-start | bytes 811016 | tf_op jit(solution)/shard_map/ppermute | solution.py:37
  74.3 7.5 %shard_map.104.refs_7_ = f32[5,192,128]{2,1,0:T(8,128)S(1)} custom-call(s32[3]{0:T(128)S(1)} %pad_add_fusion.place_ref, bf16[96,4224]{1,0:T(8,128)(2,1)S(1)} %collective-permute-done.6.refs_0_, bf16[96,4224]{1,0:T(8,128)(2,1)S(1)} %collective-permute-done.8.refs_1_, bf16[2004,4096]{1,0:T(8,128)(2,1)S(1)} %copy-done.1), custom_call_target="tpu_custom_call" | custom-call | flops 3152019456 | bytes 18038784 | tf_op jit(solution)/shard_map/pallas_call | solution.py:272
  81.8 8.5 %rest.1 = (f32[4,640]{1,0:T(4,128)S(1)}, f32[8,640]{1,0:T(8,128)S(1)}) custom-call(s32[3]{0:T(128)S(1)} %pad_add_fusion.place_ref, bf16[48,4224]{1,0:T(8,128)(2,1)S(1)} %collective-permute-done.7.refs_0_, bf16[48,4224]{1,0:T(8,128)(2,1)S(1)} %collective-permute-done.9.refs_1_, bf16[64,4224]{1,0:T(8,128)(2,1)S(1)} %collective-permute-done.13.refs_2_, ...), custom_call_target="tpu_custom_call" | custom-call | flops 4728029184 | bytes 18849792 | tf_op jit(solution)/shard_map/rest/pallas_call | solution.py:293
  90.4 19.2 %all_to_all.5.gathered = f32[64,4,640]{2,1,0:T(4,128)S(1)} all-to-all(f32[64,4,640]{2,1,0:T(4,128)S(1)} %broadcast_in_dim.32), channel_id=1, replica_groups=mesh['dp'=2,'tensor'=64] {'tensor'}, dimensions={0} | all-to-all | bytes 1310720 | tf_op jit(solution)/shard_map/all_to_all | solution.py:420
  109.6 0.9 finish.1
  (38 shorter events, 2.3 us)
Async XLA Ops:
  2.3 8.9 %collective-permute-start = (bf16[16,4224]{1,0:T(8,128)(2,1)}, bf16[16,4224]{1,0:T(8,128)(2,1)S(1)}, u32[]{:S(2)}, u32[]{:S(2)}) collective-permute-start(bf16[16,4224]{1,0:T(8,128)(2,1)} %pack.1.rows0), channel_id=1, source_target_pairs={{0,48},{1,49},{2,50},{3,51},{4,52},{5,53},{6,54},{7,55},{8,56},{9,... | collective-permute-start | bytes 405512 | tf_op jit(solution)/shard_map/ppermute | solution.py:37
  5.2 8.2 %collective-permute-start.1 = (bf16[16,4224]{1,0:T(8,128)(2,1)}, bf16[16,4224]{1,0:T(8,128)(2,1)S(1)}, u32[]{:S(2)}, u32[]{:S(2)}) collective-permute-start(bf16[16,4224]{1,0:T(8,128)(2,1)} %pack.1.rows0), channel_id=1, source_target_pairs={{0,32},{1,33},{2,34},{3,35},{4,36},{5,37},{6,38},{7,39},{8,40},{9,... | collective-permute-start | bytes 405512 | tf_op jit(solution)/shard_map/ppermute | solution.py:37
  6.0 8.9 %collective-permute-start.2 = (bf16[16,4224]{1,0:T(8,128)(2,1)}, bf16[16,4224]{1,0:T(8,128)(2,1)S(1)}, u32[]{:S(2)}, u32[]{:S(2)}) collective-permute-start(bf16[16,4224]{1,0:T(8,128)(2,1)} %pack.1.rows0), channel_id=1, source_target_pairs={{0,16},{1,17},{2,18},{3,19},{4,20},{5,21},{6,22},{7,23},{8,24},{9,... | collective-permute-start | bytes 405512 | tf_op jit(solution)/shard_map/ppermute | solution.py:37
  14.8 0.9 copy-start.2
  15.7 0.7 copy-start.3
  16.9 16.6 %collective-permute-start.3 = (bf16[24,4224]{1,0:T(8,128)(2,1)S(1)}, bf16[24,4224]{1,0:T(8,128)(2,1)S(1)}, u32[]{:S(2)}, u32[]{:S(2)}) collective-permute-start(bf16[24,4224]{1,0:T(8,128)(2,1)S(1)} %get-tuple-element.10), channel_id=1, source_target_pairs={{0,3},{1,0},{2,1},{3,2},{4,7},{5,4},{6,5},{7,6},{8,11},{9,8},{10,9... | collective-permute-start | bytes 608264 | tf_op jit(solution)/shard_map/ppermute | solution.py:37
  20.0 13.5 %collective-permute-start.4 = (bf16[24,4224]{1,0:T(8,128)(2,1)S(1)}, bf16[24,4224]{1,0:T(8,128)(2,1)S(1)}, u32[]{:S(2)}, u32[]{:S(2)}) collective-permute-start(bf16[24,4224]{1,0:T(8,128)(2,1)S(1)} %get-tuple-element.10), channel_id=1, source_target_pairs={{0,2},{1,3},{2,0},{3,1},{4,6},{5,7},{6,4},{7,5},{8,10},{9,11},{10,... | collective-permute-start | bytes 608264 | tf_op jit(solution)/shard_map/ppermute | solution.py:37
  20.7 12.9 %collective-permute-start.5 = (bf16[24,4224]{1,0:T(8,128)(2,1)S(1)}, bf16[24,4224]{1,0:T(8,128)(2,1)S(1)}, u32[]{:S(2)}, u32[]{:S(2)}) collective-permute-start(bf16[24,4224]{1,0:T(8,128)(2,1)S(1)} %get-tuple-element.10), channel_id=1, source_target_pairs={{0,1},{1,2},{2,3},{3,0},{4,5},{5,6},{6,7},{7,4},{8,9},{9,10},{10,1... | collective-permute-start | bytes 608264 | tf_op jit(solution)/shard_map/ppermute | solution.py:37
  21.6 9.0 %collective-permute-start.10 = (bf16[16,4224]{1,0:T(8,128)(2,1)S(1)}, bf16[16,4224]{1,0:T(8,128)(2,1)S(1)}, u32[]{:S(2)}, u32[]{:S(2)}) collective-permute-start(bf16[16,4224]{1,0:T(8,128)(2,1)S(1)} %get-tuple-element.11), channel_id=1, source_target_pairs={{0,12},{1,13},{2,14},{3,15},{4,0},{5,1},{6,2},{7,3},{8,4},{9,5},{1... | collective-permute-start | bytes 405512 | tf_op jit(solution)/shard_map/ppermute | solution.py:37
  26.3 6.5 %collective-permute-start.11 = (bf16[16,4224]{1,0:T(8,128)(2,1)S(1)}, bf16[16,4224]{1,0:T(8,128)(2,1)S(1)}, u32[]{:S(2)}, u32[]{:S(2)}) collective-permute-start(bf16[16,4224]{1,0:T(8,128)(2,1)S(1)} %get-tuple-element.11), channel_id=1, source_target_pairs={{0,8},{1,9},{2,10},{3,11},{4,12},{5,13},{6,14},{7,15},{8,0},{9,1},... | collective-permute-start | bytes 405512 | tf_op jit(solution)/shard_map/ppermute | solution.py:37
  30.7 6.6 %collective-permute-start.12 = (bf16[16,4224]{1,0:T(8,128)(2,1)S(1)}, bf16[16,4224]{1,0:T(8,128)(2,1)S(1)}, u32[]{:S(2)}, u32[]{:S(2)}) collective-permute-start(bf16[16,4224]{1,0:T(8,128)(2,1)S(1)} %get-tuple-element.11), channel_id=1, source_target_pairs={{0,4},{1,5},{2,6},{3,7},{4,8},{5,9},{6,10},{7,11},{8,12},{9,13},{1... | collective-permute-start | bytes 405512 | tf_op jit(solution)/shard_map/ppermute | solution.py:37
  33.6 20.4 %collective-permute-start.6 = (bf16[96,4224]{1,0:T(8,128)(2,1)S(1)}, bf16[96,4224]{1,0:T(8,128)(2,1)S(1)}, u32[]{:S(2)}, u32[]{:S(2)}) collective-permute-start(bf16[96,4224]{1,0:T(8,128)(2,1)S(1)} %constant_dynamic-update-slice_fusion.refs_0_), channel_id=1, source_target_pairs={{0,12},{1,13},{2,14},{3,15},{4,0},{5,1},{6,2},{7,3},{8,4},{9,5},{1... | collective-permute-start | bytes 2433032 | tf_op jit(solution)/shard_map/ppermute | solution.py:37
  36.6 21.3 %collective-permute-start.8 = (bf16[96,4224]{1,0:T(8,128)(2,1)S(1)}, bf16[96,4224]{1,0:T(8,128)(2,1)S(1)}, u32[]{:S(2)}, u32[]{:S(2)}) collective-permute-start(bf16[96,4224]{1,0:T(8,128)(2,1)S(1)} %constant_dynamic-update-slice_fusion.refs_0_), channel_id=1, source_target_pairs={{0,4},{1,5},{2,6},{3,7},{4,8},{5,9},{6,10},{7,11},{8,12},{9,13},{1... | collective-permute-start | bytes 2433032 | tf_op jit(solution)/shard_map/ppermute | solution.py:37
  38.0 34.1 %collective-permute-start.13 = (bf16[64,4224]{1,0:T(8,128)(2,1)}, bf16[64,4224]{1,0:T(8,128)(2,1)S(1)}, u32[]{:S(2)}, u32[]{:S(2)}) collective-permute-start(bf16[64,4224]{1,0:T(8,128)(2,1)} %constant_dynamic-update-slice_fusion.4.refs_1_), channel_id=1, source_target_pairs={{0,3},{1,0},{2,1},{3,2},{4,7},{5,4},{6,5},{7,6},{8,11},{9,8},{10,9... | collective-permute-start | bytes 1622024 | tf_op jit(solution)/shard_map/ppermute | solution.py:37
  40.2 32.5 %collective-permute-start.15 = (bf16[64,4224]{1,0:T(8,128)(2,1)}, bf16[64,4224]{1,0:T(8,128)(2,1)S(1)}, u32[]{:S(2)}, u32[]{:S(2)}) collective-permute-start(bf16[64,4224]{1,0:T(8,128)(2,1)} %constant_dynamic-update-slice_fusion.4.refs_1_), channel_id=1, source_target_pairs={{0,1},{1,2},{2,3},{3,0},{4,5},{5,6},{6,7},{7,4},{8,9},{9,10},{10,1... | collective-permute-start | bytes 1622024 | tf_op jit(solution)/shard_map/ppermute | solution.py:37
  46.0 5.6 %copy-start = (bf16[2004,4096]{1,0:T(8,128)(2,1)}, bf16[2004,4096]{1,0:T(8,128)(2,1)S(1)}, u32[]{:S(2)}) copy-start(bf16[2004,4096]{1,0:T(8,128)(2,1)S(1)} %hold.1.refs_2_.refs_8_) | copy-start | bytes 49250308
  54.1 27.7 %collective-permute-start.7 = (bf16[48,4224]{1,0:T(8,128)(2,1)S(1)}, bf16[48,4224]{1,0:T(8,128)(2,1)S(1)}, u32[]{:S(2)}, u32[]{:S(2)}) collective-permute-start(bf16[48,4224]{1,0:T(8,128)(2,1)S(1)} %slice.16), channel_id=1, source_target_pairs={{0,12},{1,13},{2,14},{3,15},{4,0},{5,1},{6,2},{7,3},{8,4},{9,5},{1... | collective-permute-start | bytes 1216520 | tf_op jit(solution)/shard_map/ppermute | solution.py:37
  57.9 23.9 %collective-permute-start.9 = (bf16[48,4224]{1,0:T(8,128)(2,1)S(1)}, bf16[48,4224]{1,0:T(8,128)(2,1)S(1)}, u32[]{:S(2)}, u32[]{:S(2)}) collective-permute-start(bf16[48,4224]{1,0:T(8,128)(2,1)S(1)} %slice.17), channel_id=1, source_target_pairs={{0,4},{1,5},{2,6},{3,7},{4,8},{5,9},{6,10},{7,11},{8,12},{9,13},{1... | collective-permute-start | bytes 1216520 | tf_op jit(solution)/shard_map/ppermute | solution.py:37
  58.0 5.7 %copy-start.1 = (bf16[2004,4096]{1,0:T(8,128)(2,1)S(1)}, bf16[2004,4096]{1,0:T(8,128)(2,1)}, u32[]{:S(2)}) copy-start(bf16[2004,4096]{1,0:T(8,128)(2,1)} %copy-done) | copy-start | bytes 49250308
  72.1 9.7 %collective-permute-start.14 = (bf16[32,4224]{1,0:T(8,128)(2,1)S(1)}, bf16[32,4224]{1,0:T(8,128)(2,1)S(1)}, u32[]{:S(2)}, u32[]{:S(2)}) collective-permute-start(bf16[32,4224]{1,0:T(8,128)(2,1)S(1)} %slice.18), channel_id=1, source_target_pairs={{0,3},{1,0},{2,1},{3,2},{4,7},{5,4},{6,5},{7,6},{8,11},{9,8},{10,9... | collective-permute-start | bytes 811016 | tf_op jit(solution)/shard_map/ppermute | solution.py:37
  72.8 36.9 %copy-start.4 = (s32[1,640]{1,0:T(1,128)S(1)}, s32[1,640]{1,0:T(1,128)}, u32[]{:S(2)}) copy-start(s32[1,640]{1,0:T(1,128)} %constant.48.clone.device) | copy-start | bytes 7684
  72.8 36.8 %copy-start.5 = (s32[12]{0:T(128)S(1)}, s32[12]{0:T(128)}, u32[]{:S(2)}) copy-start(s32[12]{0:T(128)} %param.13) | copy-start | bytes 148
  72.8 36.8 %copy-start.6 = (s32[12]{0:T(128)S(1)}, s32[12]{0:T(128)}, u32[]{:S(2)}) copy-start(s32[12]{0:T(128)} %param.12) | copy-start | bytes 148
  72.8 9.0 %collective-permute-start.16 = (bf16[32,4224]{1,0:T(8,128)(2,1)S(1)}, bf16[32,4224]{1,0:T(8,128)(2,1)S(1)}, u32[]{:S(2)}, u32[]{:S(2)}) collective-permute-start(bf16[32,4224]{1,0:T(8,128)(2,1)S(1)} %slice.19), channel_id=1, source_target_pairs={{0,1},{1,2},{2,3},{3,0},{4,5},{5,6},{6,7},{7,4},{8,9},{9,10},{10,1... | collective-permute-start | bytes 811016 | tf_op jit(solution)/shard_map/ppermute | solution.py:37

commit v2 on v1

--- a/solution.py
+++ b/solution.py
@@ -18,7 +18,7 @@
 LINE = 4 * LIVE
 ROWS_A = 24
 ROWS_B = LINE - ROWS_A
-VOCAB_TILE = 512
+VOCAB_TILE = 1024
 
 
 X, Z, Y = 0, 1, 2
@@ -43,6 +43,10 @@
 
 def in_vmem(value):
     return pltpu.with_memory_space_constraint(value, pltpu.VMEM)
+
+
+def in_hbm(value):
+    return pltpu.with_memory_space_constraint(value, pltpu.HBM)
 
 
 def pack_kernel(hidden_ref, targets_ref, mask_ref, out_ref):
@@ -101,7 +105,7 @@
         cost_estimate=pl.CostEstimate(
             flops=0, bytes_accessed=2 * head_weight.size, transcendentals=0
         ),
-    )(pltpu.with_memory_space_constraint(head_weight, pltpu.HBM))
+    )(in_hbm(head_weight))
 
 
 def prepare_kernel(own_ref, gain_ref, rows0, rows1, rows2, rows3, a_ref, b_ref):
@@ -143,6 +147,29 @@
             flops=2 * 64 * LINE * WIDE, bytes_accessed=104 * WIDE * 2, transcendentals=64
         ),
     )(own, gain, *pieces)
+
+
+def join_kernel(*refs):
+    out_ref, at = refs[-1], 0
+    for ref in refs[:-1]:
+        out_ref[at : at + ref.shape[0], :] = ref[...]
+        at += ref.shape[0]
+
+
+def join(pieces):
+    vmem = pl.BlockSpec(memory_space=pltpu.VMEM)
+    rows = sum(piece.shape[0] for piece in pieces)
+    return pl.pallas_call(
+        join_kernel,
+        name="join",
+        out_shape=jax.ShapeDtypeStruct((rows, WIDE), jnp.bfloat16),
+        in_specs=[vmem] * len(pieces),
+        out_specs=vmem,
+        compiler_params=pltpu.CompilerParams(vmem_limit_bytes=4 * 1024 * 1024),
+        cost_estimate=pl.CostEstimate(
+            flops=rows * WIDE, bytes_accessed=4 * rows * WIDE, transcendentals=0
+        ),
+    )(*[in_vmem(piece) for piece in pieces])
 
 
 def fetch(piece_refs, held, sems):
@@ -299,7 +326,7 @@
             jax.ShapeDtypeStruct((8, slots), jnp.float32),
         ),
         in_specs=[pl.BlockSpec(memory_space=pltpu.SMEM)]
-        + [pl.BlockSpec(memory_space=pl.ANY)] * len(pieces)
+        + [pl.BlockSpec(memory_space=pltpu.VMEM)] * len(pieces)
         + [
             pl.BlockSpec(near.shape, lambda i: (0, 0, 0)),
             pl.BlockSpec(side.shape, lambda i: (0, 0, 0)),
@@ -394,11 +421,13 @@
     x, z, y = me // 16, (me // 4) % 4, me % 4
     rows = pack(hidden, targets[None, :], loss_mask[None, :])
     line = [rows] + three_ahead(rows, X)
-    part_a, part_b = prepare(x[None], norm_gain[None, :], line[:1] + [in_vmem(item) for item in line[1:]])
+    part_a, part_b = prepare(
+        x[None], in_hbm(norm_gain[None, :]), [in_hbm(rows)] + [in_vmem(item) for item in line[1:]]
+    )
     row_a = [part_a] + three_ahead(part_a, Y)
     row_b = [part_b] + three_ahead(part_b, Z)
     own_a = jnp.concatenate(row_a, axis=0)
-    own_b = jnp.concatenate(row_b, axis=0)
+    own_b = join(row_b)
     up_a = from_ahead(own_a, Z, 1)
     down_a = from_ahead(own_a, Z, 3)
     up_b = from_ahead(own_b, Y, 1)
@@ -411,7 +440,7 @@
 
     place = jnp.stack([me * head_weight.shape[0], z, y])
     held_weight = hold(head_weight)
-    near = score_part(place, [own_a, own_b], held_weight)
+    near = score_part(place, [in_vmem(own_a), in_vmem(own_b)], held_weight)
     side = score_part(place, [up_a, down_a], held_weight)
     stats, info = score_rest(
         place, [*far_a, in_vmem(up_b), *far_b, in_vmem(down_b)], near, side, held_weight, na, nb

time: 111 us -> 130 us (1.17)
  waiting for transfers between devices: 16.9 us -> 41.4 us
  local copies, waits for them, and re-layouts: 15.9 us -> 12.5 us
    ppermute x17, waiting for transfers between devices: 16.9 us -> 41.4 us  [from_ahead(): return lax.ppermute(value, 'tensor', shifted_pairs(axis, step))]
    unnamed x20 -> x15, local copies, waits for them, and re-layouts: 15 us -> 11.4 us
    pallas_call x2, Pallas kernels: 15.8 us -> 14 us  [score_part(): pl.pallas_call(functools.partial(near_kernel, vocab_rows, len(pieces)), g...]
  transfers between devices with their start and end apart: 17 -> 17, of which waited for: 7 -> 9; matrix products, arithmetic and copies ran while one was open for 3% -> 1% of each run, Pallas kernels for 19% -> 15%
where the time goes in v2:
time: 130 us; the launch traced here: 129 us
  waiting for transfers between devices  41.4 us (32%)
  Pallas kernels  32.1 us (25%)
  starting transfers between devices  24.1 us (19%)
  blocking collectives  18.2 us (14%)
  local copies, waits for them, and re-layouts  12.5 us (10%)
    ppermute x17, waiting for transfers between devices, from_ahead(): return lax.ppermute(value, 'tensor', shifted_pairs(axis, step))  41.4 us
    ppermute x17, starting transfers between devices, from_ahead(): return lax.ppermute(value, 'tensor', shifted_pairs(axis, step))  24.1 us
    all_to_all x1, blocking collectives, local(): gathered = lax.all_to_all(copies, 'tensor', 0, 0, tiled=True)  18.2 us
    pallas_call x2, Pallas kernels, score_part(): pl.pallas_call(functools.partial(near_kernel, vocab_rows, len(pieces)), g...  14 us
    unnamed x15, local copies, waits for them, and re-layouts  11.4 us
    pallas_call x1, Pallas kernels, score_rest(): pl.pallas_call(functools.partial(rest_kernel, vocab_rows, len(pieces), na...  8.5 us
    pallas_call x1, Pallas kernels, hold(): pl.pallas_call(hold_kernel, name='hold', out_shape=pltpu.VMEM(head_weight...  5.68 us
  transfers between devices with their start and end apart: 17, of which 9 were waited for; matrix products, arithmetic and copies ran while one was open for 1% of the time, Pallas kernels for 15%

profile of v2, /device:TPU:0, one launch (start us, length us, event | category | flops | bytes accessed | tf_op | source)
XLA Modules:
  0.0 129.2 jit_solution(18212024324190730408)
XLA Ops:
  0.6 1.7 %pack.1.rows0 = bf16[16,4224]{1,0:T(8,128)(2,1)} custom-call(bf16[16,4096]{1,0:T(8,128)(2,1)} %hidden_ref.1, s32[1,16]{1,0:T(1,128)} %bitcast.16, s32[1,16]{1,0:T(1,128)} %bitcast.17), custom_call_target="tpu_custom_call" | custom-call | flops 67584 | bytes 270336 | tf_op jit(solution)/shard_map/pack/pallas_call | solution.py:78
  2.3 2.9 %collective-permute-start = (bf16[16,4224]{1,0:T(8,128)(2,1)}, bf16[16,4224]{1,0:T(8,128)(2,1)S(1)}, u32[]{:S(2)}, u32[]{:S(2)}) collective-permute-start(bf16[16,4224]{1,0:T(8,128)(2,1)} %pack.1.rows0), channel_id=1, source_target_pairs={{0,48},{1,49},{2,50},{3,51},{4,52},{5,53},{6,54},{7,55},{8,56},{9,... | collective-permute-start | bytes 405512 | tf_op jit(solution)/shard_map/ppermute | solution.py:37
  5.2 0.8 collective-permute-start.1
  6.0 0.9 collective-permute-start.2
  6.9 4.4 %collective-permute-done.rows1 = bf16[16,4224]{1,0:T(8,128)(2,1)S(1)} collective-permute-done((bf16[16,4224]{1,0:T(8,128)(2,1)}, bf16[16,4224]{1,0:T(8,128)(2,1)S(1)}, u32[]{:S(2)}, u32[]{:S(2)}) %collective-permute-start) | collective-permute-done | bytes 135200 | tf_op jit(solution)/shard_map/ppermute | solution.py:37
  11.2 2.1 %collective-permute-done.1.rows2 = bf16[16,4224]{1,0:T(8,128)(2,1)S(1)} collective-permute-done((bf16[16,4224]{1,0:T(8,128)(2,1)}, bf16[16,4224]{1,0:T(8,128)(2,1)S(1)}, u32[]{:S(2)}, u32[]{:S(2)}) %collective-permute-start.1) | collective-permute-done | bytes 135200 | tf_op jit(solution)/shard_map/ppermute | solution.py:37
  13.3 1.5 %collective-permute-done.2.rows3 = bf16[16,4224]{1,0:T(8,128)(2,1)S(1)} collective-permute-done((bf16[16,4224]{1,0:T(8,128)(2,1)}, bf16[16,4224]{1,0:T(8,128)(2,1)S(1)}, u32[]{:S(2)}, u32[]{:S(2)}) %collective-permute-start.2) | collective-permute-done | bytes 135200 | tf_op jit(solution)/shard_map/ppermute | solution.py:37
  14.8 1.4 %prepare.1 = (bf16[24,4224]{1,0:T(8,128)(2,1)S(1)}, bf16[16,4224]{1,0:T(8,128)(2,1)S(1)}) custom-call(s32[1]{0:T(128)} %bitcast.4.own_ref, f32[1,4096]{1,0:T(1,128)} %bitcast.15, bf16[16,4224]{1,0:T(8,128)(2,1)} %pack.1.rows0, bf16[16,4224]{1,0:T(8,128)(2,1)S(1)} %collective-permute-done.rows1, bf16[16,4224]{1,0:T(8,128)(2,1)S(1)} %collective-permute-done.1.rows2, ...), custom_call_target="tpu_custom_call" | custom-call | flops 21626880 | bytes 878592 | tf_op jit(solution)/shard_map/prepare/pallas_call | solution.py:136
  16.2 3.1 %collective-permute-start.3 = (bf16[24,4224]{1,0:T(8,128)(2,1)S(1)}, bf16[24,4224]{1,0:T(8,128)(2,1)S(1)}, u32[]{:S(2)}, u32[]{:S(2)}) collective-permute-start(bf16[24,4224]{1,0:T(8,128)(2,1)S(1)} %get-tuple-element.10), channel_id=1, source_target_pairs={{0,3},{1,0},{2,1},{3,2},{4,7},{5,4},{6,5},{7,6},{8,11},{9,8},{10,9... | collective-permute-start | bytes 608264 | tf_op jit(solution)/shard_map/ppermute | solution.py:37
  19.3 0.7 collective-permute-start.4
  20.0 1.0 collective-permute-start.5
  21.0 7.0 %collective-permute-done.3 = bf16[24,4224]{1,0:T(8,128)(2,1)S(1)} collective-permute-done((bf16[24,4224]{1,0:T(8,128)(2,1)S(1)}, bf16[24,4224]{1,0:T(8,128)(2,1)S(1)}, u32[]{:S(2)}, u32[]{:S(2)}) %collective-permute-start.3) | collective-permute-done | bytes 202784 | tf_op jit(solution)/shard_map/ppermute | solution.py:37
  28.0 0.8 collective-permute-done.4
  28.9 2.9 %collective-permute-done.5 = bf16[24,4224]{1,0:T(8,128)(2,1)S(1)} collective-permute-done((bf16[24,4224]{1,0:T(8,128)(2,1)S(1)}, bf16[24,4224]{1,0:T(8,128)(2,1)S(1)}, u32[]{:S(2)}, u32[]{:S(2)}) %collective-permute-start.5) | collective-permute-done | bytes 202784 | tf_op jit(solution)/shard_map/ppermute | solution.py:37
  31.8 4.1 %collective-permute-start.6 = (bf16[96,4224]{1,0:T(8,128)(2,1)S(1)}, bf16[96,4224]{1,0:T(8,128)(2,1)S(1)}, u32[]{:S(2)}, u32[]{:S(2)}) collective-permute-start(bf16[96,4224]{1,0:T(8,128)(2,1)S(1)} %constant_dynamic-update-slice_fusion.refs_0_), channel_id=1, source_target_pairs={{0,12},{1,13},{2,14},{3,15},{4,0},{5,1},{6,2},{7,3},{8,4},{9,5},{1... | collective-permute-start | bytes 2433032 | tf_op jit(solution)/shard_map/ppermute | solution.py:37
  35.9 3.2 %collective-permute-start.10 = (bf16[16,4224]{1,0:T(8,128)(2,1)S(1)}, bf16[16,4224]{1,0:T(8,128)(2,1)S(1)}, u32[]{:S(2)}, u32[]{:S(2)}) collective-permute-start(bf16[16,4224]{1,0:T(8,128)(2,1)S(1)} %get-tuple-element.11.refs_0_), channel_id=1, source_target_pairs={{0,12},{1,13},{2,14},{3,15},{4,0},{5,1},{6,2},{7,3},{8,4},{9,5},{1... | collective-permute-start | bytes 405512 | tf_op jit(solution)/shard_map/ppermute | solution.py:37
  39.2 0.9 collective-permute-start.12
  40.0 19.2 %collective-permute-done.10.refs_1_ = bf16[16,4224]{1,0:T(8,128)(2,1)S(1)} collective-permute-done((bf16[16,4224]{1,0:T(8,128)(2,1)S(1)}, bf16[16,4224]{1,0:T(8,128)(2,1)S(1)}, u32[]{:S(2)}, u32[]{:S(2)}) %collective-permute-start.10) | collective-permute-done | bytes 135200 | tf_op jit(solution)/shard_map/ppermute | solution.py:37
  59.6 3.0 %collective-permute-done.12.refs_3_ = bf16[16,4224]{1,0:T(8,128)(2,1)S(1)} collective-permute-done((bf16[16,4224]{1,0:T(8,128)(2,1)S(1)}, bf16[16,4224]{1,0:T(8,128)(2,1)S(1)}, u32[]{:S(2)}, u32[]{:S(2)}) %collective-permute-start.12) | collective-permute-done | bytes 135200 | tf_op jit(solution)/shard_map/ppermute | solution.py:37
  62.7 2.0 %collective-permute-start.15 = (bf16[64,4224]{1,0:T(8,128)(2,1)S(1)}, bf16[64,4224]{1,0:T(8,128)(2,1)}, u32[]{:S(2)}, u32[]{:S(2)}) collective-permute-start(bf16[64,4224]{1,0:T(8,128)(2,1)S(1)} %join.1.refs_1_), channel_id=1, source_target_pairs={{0,1},{1,2},{2,3},{3,0},{4,5},{5,6},{6,7},{7,4},{8,9},{9,10},{10,1... | collective-permute-start | bytes 1622024 | tf_op jit(solution)/shard_map/ppermute | solution.py:37
  64.8 5.7 %hold.1.refs_2_.refs_8_ = bf16[2004,4096]{1,0:T(8,128)(2,1)S(1)} custom-call(bf16[2004,4096]{1,0:T(8,128)(2,1)} %weight_ref.1), custom_call_target="tpu_custom_call" | custom-call | bytes 16416768 | tf_op jit(solution)/shard_map/hold/pallas_call | solution.py:97
  70.5 5.6 %copy-done = bf16[2004,4096]{1,0:T(8,128)(2,1)} copy-done((bf16[2004,4096]{1,0:T(8,128)(2,1)}, bf16[2004,4096]{1,0:T(8,128)(2,1)S(1)}, u32[]{:S(2)}) %copy-start) | copy-done | bytes 16416792
  76.6 1.8 %collective-permute-start.9 = (bf16[48,4224]{1,0:T(8,128)(2,1)S(1)}, bf16[48,4224]{1,0:T(8,128)(2,1)S(1)}, u32[]{:S(2)}, u32[]{:S(2)}) collective-permute-start(bf16[48,4224]{1,0:T(8,128)(2,1)S(1)} %slice.17), channel_id=1, source_target_pairs={{0,4},{1,5},{2,6},{3,7},{4,8},{5,9},{6,10},{7,11},{8,12},{9,13},{1... | collective-permute-start | bytes 1216520 | tf_op jit(solution)/shard_map/ppermute | solution.py:37
  78.4 5.7 %copy-done.1 = bf16[2004,4096]{1,0:T(8,128)(2,1)S(1)} copy-done((bf16[2004,4096]{1,0:T(8,128)(2,1)S(1)}, bf16[2004,4096]{1,0:T(8,128)(2,1)}, u32[]{:S(2)}) %copy-start.1) | copy-done | bytes 16416792
  84.1 7.0 %shard_map.103.refs_6_ = f32[5,160,128]{2,1,0:T(8,128)S(1)} custom-call(s32[3]{0:T(128)S(1)} %pad_add_fusion.place_ref, bf16[96,4224]{1,0:T(8,128)(2,1)S(1)} %constant_dynamic-update-slice_fusion.refs_0_, bf16[64,4224]{1,0:T(8,128)(2,1)S(1)} %join.1.refs_1_, bf16[2004,4096]{1,0:T(8,128)(2,1)S(1)} %copy-done.1), custom_call_target="tpu_custom_call" | custom-call | flops 2626682880 | bytes 17768448 | tf_op jit(solution)/shard_map/pallas_call | solution.py:299
  91.1 1.4 %collective-permute-start.14 = (bf16[32,4224]{1,0:T(8,128)(2,1)S(1)}, bf16[32,4224]{1,0:T(8,128)(2,1)S(1)}, u32[]{:S(2)}, u32[]{:S(2)}) collective-permute-start(bf16[32,4224]{1,0:T(8,128)(2,1)S(1)} %slice.18), channel_id=1, source_target_pairs={{0,3},{1,0},{2,1},{3,2},{4,7},{5,4},{6,5},{7,6},{8,11},{9,8},{10,9... | collective-permute-start | bytes 811016 | tf_op jit(solution)/shard_map/ppermute | solution.py:37
  92.5 1.0 slice.19
  93.5 1.0 collective-permute-start.16
  94.5 7.0 %shard_map.104.refs_7_ = f32[5,192,128]{2,1,0:T(8,128)S(1)} custom-call(s32[3]{0:T(128)S(1)} %pad_add_fusion.place_ref, bf16[96,4224]{1,0:T(8,128)(2,1)S(1)} %collective-permute-done.6.refs_0_, bf16[96,4224]{1,0:T(8,128)(2,1)S(1)} %collective-permute-done.8.refs_1_, bf16[2004,4096]{1,0:T(8,128)(2,1)S(1)} %copy-done.2), custom_call_target="tpu_custom_call" | custom-call | flops 3152019456 | bytes 18038784 | tf_op jit(solution)/shard_map/pallas_call | solution.py:299
  101.5 8.5 %rest.1 = (f32[4,640]{1,0:T(4,128)S(1)}, f32[8,640]{1,0:T(8,128)S(1)}) custom-call(s32[3]{0:T(128)S(1)} %pad_add_fusion.place_ref, bf16[48,4224]{1,0:T(8,128)(2,1)S(1)} %collective-permute-done.7.refs_0_, bf16[48,4224]{1,0:T(8,128)(2,1)S(1)} %collective-permute-done.9.refs_1_, bf16[64,4224]{1,0:T(8,128)(2,1)S(1)} %collective-permute-done.13.refs_2_, ...), custom_call_target="tpu_custom_call" | custom-call | flops 4728029184 | bytes 18849792 | tf_op jit(solution)/shard_map/rest/pallas_call | solution.py:320
  110.1 18.2 %all_to_all.5.gathered = f32[64,4,640]{2,1,0:T(4,128)S(1)} all-to-all(f32[64,4,640]{2,1,0:T(4,128)S(1)} %broadcast_in_dim.32), channel_id=1, replica_groups=mesh['dp'=2,'tensor'=64] {'tensor'}, dimensions={0} | all-to-all | bytes 1310720 | tf_op jit(solution)/shard_map/all_to_all | solution.py:449
  128.3 0.9 finish.1
  (33 shorter events, 1.2 us)
Async XLA Ops:
  2.3 8.9 %collective-permute-start = (bf16[16,4224]{1,0:T(8,128)(2,1)}, bf16[16,4224]{1,0:T(8,128)(2,1)S(1)}, u32[]{:S(2)}, u32[]{:S(2)}) collective-permute-start(bf16[16,4224]{1,0:T(8,128)(2,1)} %pack.1.rows0), channel_id=1, source_target_pairs={{0,48},{1,49},{2,50},{3,51},{4,52},{5,53},{6,54},{7,55},{8,56},{9,... | collective-permute-start | bytes 405512 | tf_op jit(solution)/shard_map/ppermute | solution.py:37
  5.2 8.2 %collective-permute-start.1 = (bf16[16,4224]{1,0:T(8,128)(2,1)}, bf16[16,4224]{1,0:T(8,128)(2,1)S(1)}, u32[]{:S(2)}, u32[]{:S(2)}) collective-permute-start(bf16[16,4224]{1,0:T(8,128)(2,1)} %pack.1.rows0), channel_id=1, source_target_pairs={{0,32},{1,33},{2,34},{3,35},{4,36},{5,37},{6,38},{7,39},{8,40},{9,... | collective-permute-start | bytes 405512 | tf_op jit(solution)/shard_map/ppermute | solution.py:37
  6.0 8.9 %collective-permute-start.2 = (bf16[16,4224]{1,0:T(8,128)(2,1)}, bf16[16,4224]{1,0:T(8,128)(2,1)S(1)}, u32[]{:S(2)}, u32[]{:S(2)}) collective-permute-start(bf16[16,4224]{1,0:T(8,128)(2,1)} %pack.1.rows0), channel_id=1, source_target_pairs={{0,16},{1,17},{2,18},{3,19},{4,20},{5,21},{6,22},{7,23},{8,24},{9,... | collective-permute-start | bytes 405512 | tf_op jit(solution)/shard_map/ppermute | solution.py:37
  16.2 11.8 %collective-permute-start.3 = (bf16[24,4224]{1,0:T(8,128)(2,1)S(1)}, bf16[24,4224]{1,0:T(8,128)(2,1)S(1)}, u32[]{:S(2)}, u32[]{:S(2)}) collective-permute-start(bf16[24,4224]{1,0:T(8,128)(2,1)S(1)} %get-tuple-element.10), channel_id=1, source_target_pairs={{0,3},{1,0},{2,1},{3,2},{4,7},{5,4},{6,5},{7,6},{8,11},{9,8},{10,9... | collective-permute-start | bytes 608264 | tf_op jit(solution)/shard_map/ppermute | solution.py:37
  19.3 9.5 %collective-permute-start.4 = (bf16[24,4224]{1,0:T(8,128)(2,1)S(1)}, bf16[24,4224]{1,0:T(8,128)(2,1)S(1)}, u32[]{:S(2)}, u32[]{:S(2)}) collective-permute-start(bf16[24,4224]{1,0:T(8,128)(2,1)S(1)} %get-tuple-element.10), channel_id=1, source_target_pairs={{0,2},{1,3},{2,0},{3,1},{4,6},{5,7},{6,4},{7,5},{8,10},{9,11},{10,... | collective-permute-start | bytes 608264 | tf_op jit(solution)/shard_map/ppermute | solution.py:37
  20.0 11.8 %collective-permute-start.5 = (bf16[24,4224]{1,0:T(8,128)(2,1)S(1)}, bf16[24,4224]{1,0:T(8,128)(2,1)S(1)}, u32[]{:S(2)}, u32[]{:S(2)}) collective-permute-start(bf16[24,4224]{1,0:T(8,128)(2,1)S(1)} %get-tuple-element.10), channel_id=1, source_target_pairs={{0,1},{1,2},{2,3},{3,0},{4,5},{5,6},{6,7},{7,4},{8,9},{9,10},{10,1... | collective-permute-start | bytes 608264 | tf_op jit(solution)/shard_map/ppermute | solution.py:37
  31.8 44.3 %collective-permute-start.6 = (bf16[96,4224]{1,0:T(8,128)(2,1)S(1)}, bf16[96,4224]{1,0:T(8,128)(2,1)S(1)}, u32[]{:S(2)}, u32[]{:S(2)}) collective-permute-start(bf16[96,4224]{1,0:T(8,128)(2,1)S(1)} %constant_dynamic-update-slice_fusion.refs_0_), channel_id=1, source_target_pairs={{0,12},{1,13},{2,14},{3,15},{4,0},{5,1},{6,2},{7,3},{8,4},{9,5},{1... | collective-permute-start | bytes 2433032 | tf_op jit(solution)/shard_map/ppermute | solution.py:37
  35.9 40.6 %collective-permute-start.8 = (bf16[96,4224]{1,0:T(8,128)(2,1)S(1)}, bf16[96,4224]{1,0:T(8,128)(2,1)S(1)}, u32[]{:S(2)}, u32[]{:S(2)}) collective-permute-start(bf16[96,4224]{1,0:T(8,128)(2,1)S(1)} %constant_dynamic-update-slice_fusion.refs_0_), channel_id=1, source_target_pairs={{0,4},{1,5},{2,6},{3,7},{4,8},{5,9},{6,10},{7,11},{8,12},{9,13},{1... | collective-permute-start | bytes 2433032 | tf_op jit(solution)/shard_map/ppermute | solution.py:37
  35.9 23.3 %collective-permute-start.10 = (bf16[16,4224]{1,0:T(8,128)(2,1)S(1)}, bf16[16,4224]{1,0:T(8,128)(2,1)S(1)}, u32[]{:S(2)}, u32[]{:S(2)}) collective-permute-start(bf16[16,4224]{1,0:T(8,128)(2,1)S(1)} %get-tuple-element.11.refs_0_), channel_id=1, source_target_pairs={{0,12},{1,13},{2,14},{3,15},{4,0},{5,1},{6,2},{7,3},{8,4},{9,5},{1... | collective-permute-start | bytes 405512 | tf_op jit(solution)/shard_map/ppermute | solution.py:37
  39.1 20.4 %collective-permute-start.11 = (bf16[16,4224]{1,0:T(8,128)(2,1)S(1)}, bf16[16,4224]{1,0:T(8,128)(2,1)S(1)}, u32[]{:S(2)}, u32[]{:S(2)}) collective-permute-start(bf16[16,4224]{1,0:T(8,128)(2,1)S(1)} %get-tuple-element.11.refs_0_), channel_id=1, source_target_pairs={{0,8},{1,9},{2,10},{3,11},{4,12},{5,13},{6,14},{7,15},{8,0},{9,1},... | collective-permute-start | bytes 405512 | tf_op jit(solution)/shard_map/ppermute | solution.py:37
  39.2 23.5 %collective-permute-start.12 = (bf16[16,4224]{1,0:T(8,128)(2,1)S(1)}, bf16[16,4224]{1,0:T(8,128)(2,1)S(1)}, u32[]{:S(2)}, u32[]{:S(2)}) collective-permute-start(bf16[16,4224]{1,0:T(8,128)(2,1)S(1)} %get-tuple-element.11.refs_0_), channel_id=1, source_target_pairs={{0,4},{1,5},{2,6},{3,7},{4,8},{5,9},{6,10},{7,11},{8,12},{9,13},{1... | collective-permute-start | bytes 405512 | tf_op jit(solution)/shard_map/ppermute | solution.py:37
  62.7 28.4 %collective-permute-start.13 = (bf16[64,4224]{1,0:T(8,128)(2,1)S(1)}, bf16[64,4224]{1,0:T(8,128)(2,1)S(1)}, u32[]{:S(2)}, u32[]{:S(2)}) collective-permute-start(bf16[64,4224]{1,0:T(8,128)(2,1)S(1)} %join.1.refs_1_), channel_id=1, source_target_pairs={{0,3},{1,0},{2,1},{3,2},{4,7},{5,4},{6,5},{7,6},{8,11},{9,8},{10,9... | collective-permute-start | bytes 1622024 | tf_op jit(solution)/shard_map/ppermute | solution.py:37
  62.7 29.7 %collective-permute-start.15 = (bf16[64,4224]{1,0:T(8,128)(2,1)S(1)}, bf16[64,4224]{1,0:T(8,128)(2,1)}, u32[]{:S(2)}, u32[]{:S(2)}) collective-permute-start(bf16[64,4224]{1,0:T(8,128)(2,1)S(1)} %join.1.refs_1_), channel_id=1, source_target_pairs={{0,1},{1,2},{2,3},{3,0},{4,5},{5,6},{6,7},{7,4},{8,9},{9,10},{10,1... | collective-permute-start | bytes 1622024 | tf_op jit(solution)/shard_map/ppermute | solution.py:37
  70.5 5.6 %copy-start = (bf16[2004,4096]{1,0:T(8,128)(2,1)}, bf16[2004,4096]{1,0:T(8,128)(2,1)S(1)}, u32[]{:S(2)}) copy-start(bf16[2004,4096]{1,0:T(8,128)(2,1)S(1)} %hold.1.refs_2_.refs_8_) | copy-start | bytes 49250308
  76.2 25.3 %collective-permute-start.7 = (bf16[48,4224]{1,0:T(8,128)(2,1)S(1)}, bf16[48,4224]{1,0:T(8,128)(2,1)S(1)}, u32[]{:S(2)}, u32[]{:S(2)}) collective-permute-start(bf16[48,4224]{1,0:T(8,128)(2,1)S(1)} %slice.16), channel_id=1, source_target_pairs={{0,12},{1,13},{2,14},{3,15},{4,0},{5,1},{6,2},{7,3},{8,4},{9,5},{1... | collective-permute-start | bytes 1216520 | tf_op jit(solution)/shard_map/ppermute | solution.py:37
  76.6 25.0 %collective-permute-start.9 = (bf16[48,4224]{1,0:T(8,128)(2,1)S(1)}, bf16[48,4224]{1,0:T(8,128)(2,1)S(1)}, u32[]{:S(2)}, u32[]{:S(2)}) collective-permute-start(bf16[48,4224]{1,0:T(8,128)(2,1)S(1)} %slice.17), channel_id=1, source_target_pairs={{0,4},{1,5},{2,6},{3,7},{4,8},{5,9},{6,10},{7,11},{8,12},{9,13},{1... | collective-permute-start | bytes 1216520 | tf_op jit(solution)/shard_map/ppermute | solution.py:37
  78.4 5.7 %copy-start.1 = (bf16[2004,4096]{1,0:T(8,128)(2,1)S(1)}, bf16[2004,4096]{1,0:T(8,128)(2,1)}, u32[]{:S(2)}) copy-start(bf16[2004,4096]{1,0:T(8,128)(2,1)} %copy-done) | copy-start | bytes 49250308
  84.1 10.4 %copy-start.2 = (bf16[2004,4096]{1,0:T(8,128)(2,1)S(1)}, bf16[2004,4096]{1,0:T(8,128)(2,1)}, u32[]{:S(2)}) copy-start(bf16[2004,4096]{1,0:T(8,128)(2,1)} %copy-done) | copy-start | bytes 49250308
  91.1 10.4 %collective-permute-start.14 = (bf16[32,4224]{1,0:T(8,128)(2,1)S(1)}, bf16[32,4224]{1,0:T(8,128)(2,1)S(1)}, u32[]{:S(2)}, u32[]{:S(2)}) collective-permute-start(bf16[32,4224]{1,0:T(8,128)(2,1)S(1)} %slice.18), channel_id=1, source_target_pairs={{0,3},{1,0},{2,1},{3,2},{4,7},{5,4},{6,5},{7,6},{8,11},{9,8},{10,9... | collective-permute-start | bytes 811016 | tf_op jit(solution)/shard_map/ppermute | solution.py:37
  93.5 34.9 %copy-start.3 = (s32[1,640]{1,0:T(1,128)S(1)}, s32[1,640]{1,0:T(1,128)}, u32[]{:S(2)}) copy-start(s32[1,640]{1,0:T(1,128)} %constant.48.clone.device) | copy-start | bytes 7684
  93.5 34.9 %copy-start.4 = (s32[12]{0:T(128)S(1)}, s32[12]{0:T(128)}, u32[]{:S(2)}) copy-start(s32[12]{0:T(128)} %param.13) | copy-start | bytes 148
  93.5 34.8 %copy-start.5 = (s32[12]{0:T(128)S(1)}, s32[12]{0:T(128)}, u32[]{:S(2)}) copy-start(s32[12]{0:T(128)} %param.12) | copy-start | bytes 148
  93.5 8.0 %collective-permute-start.16 = (bf16[32,4224]{1,0:T(8,128)(2,1)S(1)}, bf16[32,4224]{1,0:T(8,128)(2,1)S(1)}, u32[]{:S(2)}, u32[]{:S(2)}) collective-permute-start(bf16[32,4224]{1,0:T(8,128)(2,1)S(1)} %slice.19), channel_id=1, source_target_pairs={{0,1},{1,2},{2,3},{3,0},{4,5},{5,6},{6,7},{7,4},{8,9},{9,10},{10,1... | collective-permute-start | bytes 811016 | tf_op jit(solution)/shard_map/ppermute | solution.py:37
